TPU v7x, 512 devices: a whole 4x4x16 slice. The times are simulated.
512 devices in a mesh: ctx: 64 (over y, z), tp: 8 (over x, core).
Axes of the slice: x: 4, y: 4, z: 16, core: 2. Of those that a mesh axis runs over, the one named last changes fastest.
Arguments:
- queries: bfloat16 [16384, 4096], P('ctx', 'tp'), may hold values from -112 to 112
- keys: bfloat16 [16384, 1024], P('ctx', 'tp'), may hold values from -4.5 to 4.5
- values: bfloat16 [16384, 1024], P('ctx', 'tp'), may hold values from -6 to 6
- head_kind: int32 [8], replicated, may hold values from 0 to 1, as said below
- sink_len: int32 [8], replicated, may hold values from 32 to 128, as said below
- window_len: int32 [8], replicated, may hold values from 512 to 1024, as said below
- w_out: bfloat16 [4096, 4096], P('tp'), may hold values from -0.375 to 0.375
Outputs:
- mixed: bfloat16 [16384, 4096], P(('ctx', 'tp'))
Inputs may be any that keep to these rules, and one draw needn't show every extreme that they name: `head_kind`: exactly 4 entries are 1. `sink_len`: some head with head_kind 0 has exactly 128. `window_len`: some head with head_kind 0 has exactly 1024.
All inputs are finite; a program needn't handle non-finite values.
Results may differ from a plain program's by a relative error of at most 0.014.
Values may be sent and summed in bfloat16 or wider, within the bound.
No kernel may reach another device: no remote copies, remote signals or barrier semaphores. Data moves between devices by JAX's collectives and lax.ppermute only.
A program may use at most 64 MiB of HBM per device.

v0:
```python
import functools
import math

import jax
import jax.numpy as jnp
from jax import lax
from jax.experimental import pallas as pl
from jax.experimental.pallas import tpu as pltpu
from jax.sharding import Mesh
from jax.sharding import PartitionSpec as P


HD = 128
GROUP = 4
NY, NZ, NX, NC = 4, 16, 4, 2
ROWS = 256
ROW_KEYS = NZ * ROWS
LOW = -1e30
MASKED = -3e30
SCALE = 1.0 / math.sqrt(HD)
EXP2_SCALE = SCALE * math.log2(math.e)
STAT_ROWS = 16
PACK = GROUP * HD + STAT_ROWS
NT = (((1,), (1,)), ((), ()))


def pack_kernel(k_ref, v_ref, out_ref):
    out_ref[:, :HD] = k_ref[...]
    for half in range(2):
        rows = slice(half * HD, (half + 1) * HD)
        out_ref[rows, HD:] = v_ref[rows, :].astype(jnp.float32).T.astype(jnp.bfloat16)


def order_kernel(q_ref, out_ref):
    for x in range(NX):
        for c in range(NC):
            to, at = c * 128 + x * 32, (x * NC + c) * 32
            out_ref[to : to + 32, :] = q_ref[at : at + 32, :]


def query_offsets(shape):
    col = lax.broadcasted_iota(jnp.int32, shape, 1)
    return ((col % 128) // 32 * NC + col // 128) * 32 + col % 32


def fold(q_ref, slot, keys, values, mask, valid, acc, top, total):
    def score(h):
        q = q_ref[slot, :, h * HD : (h + 1) * HD]
        out = []
        for k in keys:
            s = lax.dot_general(k, q, NT, preferred_element_type=jnp.float32)
            out.append(s if mask is None else jnp.where(mask, s, MASKED))
        return out

    def peaks(h, scores):
        new = top[slot, h]
        for n, s in enumerate(scores):
            peak = jnp.max(s.reshape(ROWS // 8, 8, ROWS), axis=0)
            peak = jnp.max(peak, axis=0, keepdims=True)
            if valid is not None:
                peak = jnp.where(valid[n], peak, LOW)
            new = jnp.maximum(new, peak)
        return new

    scores = score(0)
    new = peaks(0, scores)
    for h in range(GROUP):
        if h + 1 < GROUP:
            scores_next = score(h + 1)
            new_next = peaks(h + 1, scores_next)
        old = top[slot, h]
        factor = jnp.exp2((old - new) * EXP2_SCALE)
        part = total[slot, h] * factor
        weights = []
        for n, s in enumerate(scores):
            shift = new[:1] * EXP2_SCALE
            if valid is not None:
                shift = jnp.where(valid[n], shift, -MASKED)
            w = jnp.exp2(s * EXP2_SCALE - shift)
            part = part + jnp.sum(w.reshape(ROWS // 8, 8, ROWS), axis=0)
            weights.append(w.astype(jnp.bfloat16))
        out = jnp.dot(
            jnp.concatenate(values, axis=1),
            jnp.concatenate(weights, axis=0),
            preferred_element_type=jnp.float32,
        )
        top[slot, h] = new
        total[slot, h] = part
        acc[slot, h] = acc[slot, h] * factor[:1] + out
        if h + 1 < GROUP:
            scores, new = scores_next, new_next


def split_block(block_ref, k_ref, v_ref):
    k_ref[...] = block_ref[:, :HD]
    v_ref[:, :HD] = block_ref[:HD, HD:]
    v_ref[:, HD:] = block_ref[HD:, HD:]


def fold_masked(info, q_ref, slot, k_ref, v_ref, key_start, acc, top, total):
    kind, sink, window = info[2], info[3], info[4]
    query_start = (info[0] + slot) * ROW_KEYS + info[1] * ROWS
    needed = (key_start <= query_start + ROWS - 1) & (
        (kind == 1) | (key_start + ROWS - 1 > query_start - window) | (key_start < sink)
    )

    @pl.when(needed)
    def _():
        i = query_start + query_offsets((ROWS, ROWS))
        j = key_start + lax.broadcasted_iota(jnp.int32, (ROWS, ROWS), 0)
        mask = (j <= i) & ((kind == 1) | (j > i - window) | (j < sink))
        fold(q_ref, slot, [k_ref[...]], [v_ref[...]], mask, None, acc, top, total)


def first_kernel(kinds, sinks, windows, q_ref, own_ref, acc, top, total, k_ref, v_ref):
    info = read_info((kinds, sinks, windows))
    acc[...] = jnp.zeros_like(acc)
    top[...] = jnp.full_like(top, LOW)
    total[...] = jnp.zeros_like(total)
    own_start = info[0] * ROW_KEYS + info[1] * ROWS
    split_block(own_ref, k_ref, v_ref)
    fold_masked(info, q_ref, 0, k_ref, v_ref, own_start, acc, top, total)


def step_kernel(
    distance, last, kinds, sinks, windows, q0_ref, q1_ref, q2_ref, q3_ref, a_ref, b_ref,
    acc_in, top_in, total_in, acc, top, total, q_ref, k_ref, v_ref
):
    del acc_in, top_in, total_in
    info = read_info((kinds, sinks, windows))
    y, z, kind = info[0], info[1], info[2]
    slots = NY - y
    a_place = lax.rem(z - distance + NZ, NZ)
    b_place = lax.rem(z + (0 if last else distance), NZ)
    q_ref[0] = q0_ref[...]
    q_ref[1] = q1_ref[...]
    q_ref[2] = q2_ref[...]
    q_ref[3] = q3_ref[...]
    split_block(a_ref, k_ref.at[0], v_ref.at[0])
    split_block(b_ref, k_ref.at[1], v_ref.at[1])
    a_before = a_place < z
    b_before = b_place < z

    @pl.when(kind == 1)
    def _():
        @pl.loop(jnp.where(a_before | b_before, 0, 1), slots)
        def _(slot):
            valid = [(slot > 0) | a_before, (slot > 0) | b_before]
            fold(q_ref, slot, [k_ref[0], k_ref[1]], [v_ref[0], v_ref[1]], None, valid, acc, top, total)

    @pl.when(kind != 1)
    def _():
        @pl.loop(0, 2 * slots)
        def _(n):
            slot = n // 2
            side = n % 2
            place = jnp.where(side == 0, a_place, b_place)
            skip = (slot == 0) & (place == z)

            @pl.when(jnp.logical_not(skip))
            def _():
                key_start = y * ROW_KEYS + place * ROWS
                fold_masked(info, q_ref, slot, k_ref.at[side], v_ref.at[side], key_start, acc, top, total)


def finish_kernel(acc, top, total, out_ref):
    y = lax.axis_index("y")
    for target in range(NY):
        slot = jnp.maximum(target - y, 0)
        valid = target >= y
        parts = []
        for h in range(GROUP):
            s = jnp.sum(total[slot, h], axis=0, keepdims=True)
            have = (s > 0.0) & valid
            safe = jnp.where(have, s, 1.0)
            o = jnp.where(have, acc[slot, h] * (1.0 / safe), 0.0).astype(jnp.bfloat16)
            lse = jnp.where(have, top[slot, h][:1] * SCALE + jnp.log(safe), LOW)
            for c in range(NC):
                out_ref[target * NC + c, h * HD : (h + 1) * HD, :] = o[:, c * 128 : (c + 1) * 128]
            high = lse.astype(jnp.bfloat16).astype(jnp.float32)
            rest = lse - high
            mid = rest.astype(jnp.bfloat16).astype(jnp.float32)
            parts += [high, mid, rest - mid]
        parts += [jnp.zeros_like(parts[0])] * (STAT_ROWS - len(parts))
        packed = jnp.concatenate(parts, axis=0).astype(jnp.bfloat16)
        for c in range(NC):
            out_ref[target * NC + c, GROUP * HD :, :] = packed[:, c * 128 : (c + 1) * 128]


def project_kernel(parts_ref, own_w_ref, other_w_ref, out_ref, mix):
    @pl.when(pl.program_id(0) == 0)
    def _():
        core = lax.axis_index("core")
        for side in range(NC):
            source = core if side == 0 else 1 - core
            stats = [
                parts_ref[y * NC + source, GROUP * HD :, :].astype(jnp.float32) for y in range(NY)
            ]
            for h in range(GROUP):
                lse = [s[3 * h : 3 * h + 1] + s[3 * h + 1 : 3 * h + 2] + s[3 * h + 2 : 3 * h + 3] for s in stats]
                peak = functools.reduce(jnp.maximum, lse)
                weight = [jnp.exp(v - peak) for v in lse]
                norm = 1.0 / functools.reduce(jnp.add, weight)
                out = None
                for y in range(NY):
                    o = parts_ref[y * NC + source, h * HD : (h + 1) * HD, :].astype(jnp.float32)
                    o = o * (weight[y] * norm)
                    out = o if out is None else out + o
                mix[side, :, h * HD : (h + 1) * HD] = out.T.astype(jnp.bfloat16)

    out_ref[...] = (
        jnp.dot(mix[0], own_w_ref[...], preferred_element_type=jnp.float32)
        + jnp.dot(mix[1], other_w_ref[...], preferred_element_type=jnp.float32)
    ).astype(jnp.bfloat16)


def read_info(heads):
    y, z = lax.axis_index("y"), lax.axis_index("z")
    core = lax.axis_index("core")
    head = lax.axis_index("x") * NC + core
    return (y, z, *(table[head] for table in heads), core)


VMEM_SPEC = pl.BlockSpec(memory_space=pltpu.VMEM)
SMEM_SPEC = pl.BlockSpec(memory_space=pltpu.SMEM)
STATE = [
    jax.ShapeDtypeStruct((NY, GROUP, HD, ROWS), jnp.float32),
    jax.ShapeDtypeStruct((NY, GROUP, 8, ROWS), jnp.float32),
    jax.ShapeDtypeStruct((NY, GROUP, 8, ROWS), jnp.float32),
]


def params(mib=24):
    return pltpu.CompilerParams(vmem_limit_bytes=mib << 20)


def body(queries, keys, values, head_kind, sink_len, window_len, w_out):
    heads = (head_kind, sink_len, window_len)
    own = pl.pallas_call(
        pack_kernel,
        out_shape=jax.ShapeDtypeStruct((ROWS, 2 * HD), jnp.bfloat16),
        in_specs=[VMEM_SPEC] * 2,
        out_specs=VMEM_SPEC,
        compiler_params=params(),
        name="pack",
    )(keys, values)
    queries = pl.pallas_call(
        order_kernel,
        out_shape=jax.ShapeDtypeStruct(queries.shape, jnp.bfloat16),
        in_specs=[VMEM_SPEC],
        out_specs=VMEM_SPEC,
        compiler_params=params(),
        name="order",
    )(queries)

    ahead = [(i, (i + 1) % NZ) for i in range(NZ)]
    behind = [(i, (i - 1) % NZ) for i in range(NZ)]
    half = NZ // 2
    a, b = {0: own}, {0: own}
    cost = pl.CostEstimate(flops=1 << 30, bytes_accessed=8 << 20, transcendentals=1 << 22)
    state = pl.pallas_call(
        first_kernel,
        out_shape=STATE,
        in_specs=[SMEM_SPEC] * 3 + [VMEM_SPEC] * 2,
        out_specs=[VMEM_SPEC] * 3,
        scratch_shapes=[pltpu.VMEM((ROWS, HD), jnp.bfloat16), pltpu.VMEM((HD, ROWS), jnp.bfloat16)],
        compiler_params=params(),
        cost_estimate=cost,
        name="first",
    )(*heads, queries[None], own)

    for d in range(1, half + 1):
        a[d] = lax.ppermute(a[d - 1], "z", ahead)
        if d < half:
            b[d] = lax.ppermute(b[d - 1], "z", behind)
    b[half] = own
    received = []
    for k in range(1, NY):
        received.append(lax.ppermute(queries, "y", [(i, i - k) for i in range(k, NY)]))
    other_w = lax.ppermute(w_out, "core", [(0, 1), (1, 0)])

    for d in range(1, half + 1):
        state = pl.pallas_call(
            functools.partial(step_kernel, d, d == half),
            out_shape=STATE,
            in_specs=[SMEM_SPEC] * 3 + [VMEM_SPEC] * 9,
            out_specs=[VMEM_SPEC] * 3,
            scratch_shapes=[
                pltpu.VMEM((NY, ROWS, GROUP * HD), jnp.bfloat16),
                pltpu.VMEM((2, ROWS, HD), jnp.bfloat16),
                pltpu.VMEM((2, HD, ROWS), jnp.bfloat16),
            ],
            input_output_aliases={9: 0, 10: 1, 11: 2},
            compiler_params=params(),
            cost_estimate=cost,
            name="step",
        )(*heads, queries, *received, a[d], b[d], *state)

    packed = pl.pallas_call(
        finish_kernel,
        out_shape=jax.ShapeDtypeStruct((NY * NC, PACK, ROWS // NC), jnp.bfloat16),
        in_specs=[VMEM_SPEC] * 3,
        out_specs=VMEM_SPEC,
        compiler_params=params(),
        name="finish",
    )(*state)
    parts = lax.all_to_all(packed, ("y", "core"), 0, 0, tiled=True)

    width = 1024
    mixed = pl.pallas_call(
        project_kernel,
        out_shape=jax.ShapeDtypeStruct((ROWS // NC, w_out.shape[1]), jnp.bfloat16),
        grid=(w_out.shape[1] // width,),
        in_specs=[
            VMEM_SPEC,
            pl.BlockSpec((GROUP * HD, width), lambda i: (0, i)),
            pl.BlockSpec((GROUP * HD, width), lambda i: (0, i)),
        ],
        out_specs=pl.BlockSpec((ROWS // NC, width), lambda i: (0, i)),
        scratch_shapes=[pltpu.VMEM((NC, ROWS // NC, GROUP * HD), jnp.bfloat16)],
        compiler_params=params(),
        name="project",
    )(parts, w_out, other_w)
    pieces = lax.all_to_all(mixed.reshape(NX, 32, -1), "x", 0, 0, tiled=True)
    return jnp.sum(pieces.astype(jnp.float32), axis=0).astype(jnp.bfloat16)


def solution(mesh):
    grid = Mesh(mesh.devices.reshape(NY, NZ, NX, NC), ("y", "z", "x", "core"))
    tokens, heads = ("y", "z"), ("x", "core")
    split = P(tokens, heads)

    return jax.shard_map(
        body,
        mesh=grid,
        in_specs=(split, split, split, P(), P(), P(), P(heads, None)),
        out_specs=P(tokens + heads, None),
        check_vma=False,
    )
```

profile of v0, /device:TPU:224, one launch (start us, length us, event | category | flops | bytes accessed | tf_op | source)
XLA Modules:
  0.0 151.6 jit_solution(6300492546040959925)
XLA Ops:
  0.0 1.9 %collective-permute-start.18 = (bf16[512,4096]{1,0:T(8,128)(2,1)}, bf16[512,4096]{1,0:T(8,128)(2,1)S(1)}, u32[]{:S(2)}, u32[]{:S(2)}) collective-permute-start(bf16[512,4096]{1,0:T(8,128)(2,1)} %own_w_ref.1), channel_id=1, source_target_pairs={{0,1},{1,0},{2,3},{3,2},{4,5},{5,4},{6,7},{7,6},{8,9},{9,8},{10,11... | collective-permute-start | bytes 12582920 | tf_op jit(solution)/shard_map/ppermute | solution.py:280
  3.7 5.0 %collective-permute-start.3 = (bf16[256,256]{1,0:T(8,128)(2,1)S(1)}, bf16[256,256]{1,0:T(8,128)(2,1)S(1)}, u32[]{:S(2)}, u32[]{:S(2)}) collective-permute-start(bf16[256,256]{1,0:T(8,128)(2,1)S(1)} %pack.1.own_ref.b_ref), channel_id=1, source_target_pairs={{0,8},{8,16},{16,24},{24,32},{32,40},{40,48},{48,56},{56,64},{64,7... | collective-permute-start | bytes 393224 | tf_op jit(solution)/shard_map/ppermute | solution.py:273
  8.7 1.9 %collective-permute-start.11 = (bf16[256,256]{1,0:T(8,128)(2,1)S(1)}, bf16[256,256]{1,0:T(8,128)(2,1)S(1)}, u32[]{:S(2)}, u32[]{:S(2)}) collective-permute-start(bf16[256,256]{1,0:T(8,128)(2,1)S(1)} %pack.1.own_ref.b_ref), channel_id=1, source_target_pairs={{0,120},{8,0},{16,8},{24,16},{32,24},{40,32},{48,40},{56,48},{64,5... | collective-permute-start | bytes 393224 | tf_op jit(solution)/shard_map/ppermute | solution.py:275
  13.0 5.1 %collective-permute-start.4 = (bf16[256,256]{1,0:T(8,128)(2,1)S(1)}, bf16[256,256]{1,0:T(8,128)(2,1)S(1)}, u32[]{:S(2)}, u32[]{:S(2)}) collective-permute-start(bf16[256,256]{1,0:T(8,128)(2,1)S(1)} %collective-permute-done.3.a_ref), channel_id=1, source_target_pairs={{0,8},{8,16},{16,24},{24,32},{32,40},{40,48},{48,56},{56,64},{64,7... | collective-permute-start | bytes 393224 | tf_op jit(solution)/shard_map/ppermute | solution.py:273
  18.1 1.9 %collective-permute-start.12 = (bf16[256,256]{1,0:T(8,128)(2,1)S(1)}, bf16[256,256]{1,0:T(8,128)(2,1)S(1)}, u32[]{:S(2)}, u32[]{:S(2)}) collective-permute-start(bf16[256,256]{1,0:T(8,128)(2,1)S(1)} %collective-permute-done.11.b_ref), channel_id=1, source_target_pairs={{0,120},{8,0},{16,8},{24,16},{32,24},{40,32},{48,40},{56,48},{64,5... | collective-permute-start | bytes 393224 | tf_op jit(solution)/shard_map/ppermute | solution.py:275
  20.9 5.6 %collective-permute-start.5 = (bf16[256,256]{1,0:T(8,128)(2,1)S(1)}, bf16[256,256]{1,0:T(8,128)(2,1)S(1)}, u32[]{:S(2)}, u32[]{:S(2)}) collective-permute-start(bf16[256,256]{1,0:T(8,128)(2,1)S(1)} %collective-permute-done.4.a_ref), channel_id=1, source_target_pairs={{0,8},{8,16},{16,24},{24,32},{32,40},{40,48},{48,56},{56,64},{64,7... | collective-permute-start | bytes 393224 | tf_op jit(solution)/shard_map/ppermute | solution.py:273
  26.5 1.9 %collective-permute-start.13 = (bf16[256,256]{1,0:T(8,128)(2,1)S(1)}, bf16[256,256]{1,0:T(8,128)(2,1)S(1)}, u32[]{:S(2)}, u32[]{:S(2)}) collective-permute-start(bf16[256,256]{1,0:T(8,128)(2,1)S(1)} %collective-permute-done.12.b_ref), channel_id=1, source_target_pairs={{0,120},{8,0},{16,8},{24,16},{32,24},{40,32},{48,40},{56,48},{64,5... | collective-permute-start | bytes 393224 | tf_op jit(solution)/shard_map/ppermute | solution.py:275
  31.1 5.1 %collective-permute-start.6 = (bf16[256,256]{1,0:T(8,128)(2,1)S(1)}, bf16[256,256]{1,0:T(8,128)(2,1)S(1)}, u32[]{:S(2)}, u32[]{:S(2)}) collective-permute-start(bf16[256,256]{1,0:T(8,128)(2,1)S(1)} %collective-permute-done.5.a_ref), channel_id=1, source_target_pairs={{0,8},{8,16},{16,24},{24,32},{32,40},{40,48},{48,56},{56,64},{64,7... | collective-permute-start | bytes 393224 | tf_op jit(solution)/shard_map/ppermute | solution.py:273
  36.2 1.9 %collective-permute-start.14 = (bf16[256,256]{1,0:T(8,128)(2,1)S(1)}, bf16[256,256]{1,0:T(8,128)(2,1)S(1)}, u32[]{:S(2)}, u32[]{:S(2)}) collective-permute-start(bf16[256,256]{1,0:T(8,128)(2,1)S(1)} %collective-permute-done.13.b_ref), channel_id=1, source_target_pairs={{0,120},{8,0},{16,8},{24,16},{32,24},{40,32},{48,40},{56,48},{64,5... | collective-permute-start | bytes 393224 | tf_op jit(solution)/shard_map/ppermute | solution.py:275
  38.7 5.6 %collective-permute-start.7 = (bf16[256,256]{1,0:T(8,128)(2,1)S(1)}, bf16[256,256]{1,0:T(8,128)(2,1)S(1)}, u32[]{:S(2)}, u32[]{:S(2)}) collective-permute-start(bf16[256,256]{1,0:T(8,128)(2,1)S(1)} %collective-permute-done.6.a_ref), channel_id=1, source_target_pairs={{0,8},{8,16},{16,24},{24,32},{32,40},{40,48},{48,56},{56,64},{64,7... | collective-permute-start | bytes 393224 | tf_op jit(solution)/shard_map/ppermute | solution.py:273
  47.9 1.9 %collective-permute-start.15 = (bf16[256,256]{1,0:T(8,128)(2,1)S(1)}, bf16[256,256]{1,0:T(8,128)(2,1)S(1)}, u32[]{:S(2)}, u32[]{:S(2)}) collective-permute-start(bf16[256,256]{1,0:T(8,128)(2,1)S(1)} %collective-permute-done.14.b_ref), channel_id=1, source_target_pairs={{0,120},{8,0},{16,8},{24,16},{32,24},{40,32},{48,40},{56,48},{64,5... | collective-permute-start | bytes 393224 | tf_op jit(solution)/shard_map/ppermute | solution.py:275
  49.8 1.7 %step.8 = (f32[4,4,128,256]{3,2,1,0:T(8,128)S(1)}, f32[4,4,8,256]{3,2,1,0:T(8,128)S(1)}, f32[4,4,8,256]{3,2,1,0:T(8,128)S(1)}) custom-call(s32[8]{0:T(128)S(1)} %copy-done.4, s32[8]{0:T(128)S(1)} %copy-done.5, s32[8]{0:T(128)S(1)} %copy-done.6, bf16[256,512]{1,0:T(8,128)(2,1)S(1)} %order.1.q0_ref, ...), custom_call_target="tpu_custom_call", output_to_operand_aliasing={{0}: (9, {}), {1}: (10, {}), {2}: (11, {})} | custom-call | flops 1073741824 | bytes 8388608 | tf_op jit(solution)/shard_map/step/pallas_call | solution.py:283
  51.6 5.1 %collective-permute-start.8 = (bf16[256,256]{1,0:T(8,128)(2,1)S(1)}, bf16[256,256]{1,0:T(8,128)(2,1)S(1)}, u32[]{:S(2)}, u32[]{:S(2)}) collective-permute-start(bf16[256,256]{1,0:T(8,128)(2,1)S(1)} %collective-permute-done.7.a_ref), channel_id=1, source_target_pairs={{0,8},{8,16},{16,24},{24,32},{32,40},{40,48},{48,56},{56,64},{64,7... | collective-permute-start | bytes 393224 | tf_op jit(solution)/shard_map/ppermute | solution.py:273
  56.7 1.7 %step.9 = (f32[4,4,128,256]{3,2,1,0:T(8,128)S(1)}, f32[4,4,8,256]{3,2,1,0:T(8,128)S(1)}, f32[4,4,8,256]{3,2,1,0:T(8,128)S(1)}) custom-call(s32[8]{0:T(128)S(1)} %copy-done.4, s32[8]{0:T(128)S(1)} %copy-done.5, s32[8]{0:T(128)S(1)} %copy-done.6, bf16[256,512]{1,0:T(8,128)(2,1)S(1)} %order.1.q0_ref, ...), custom_call_target="tpu_custom_call", output_to_operand_aliasing={{0}: (9, {}), {1}: (10, {}), {2}: (11, {})} | custom-call | flops 1073741824 | bytes 8388608 | tf_op jit(solution)/shard_map/step/pallas_call | solution.py:283
  58.5 1.9 %collective-permute-start.16 = (bf16[256,256]{1,0:T(8,128)(2,1)S(1)}, bf16[256,256]{1,0:T(8,128)(2,1)S(1)}, u32[]{:S(2)}, u32[]{:S(2)}) collective-permute-start(bf16[256,256]{1,0:T(8,128)(2,1)S(1)} %collective-permute-done.15.b_ref), channel_id=1, source_target_pairs={{0,120},{8,0},{16,8},{24,16},{32,24},{40,32},{48,40},{56,48},{64,5... | collective-permute-start | bytes 393224 | tf_op jit(solution)/shard_map/ppermute | solution.py:275
  60.4 1.7 %step.10 = (f32[4,4,128,256]{3,2,1,0:T(8,128)S(1)}, f32[4,4,8,256]{3,2,1,0:T(8,128)S(1)}, f32[4,4,8,256]{3,2,1,0:T(8,128)S(1)}) custom-call(s32[8]{0:T(128)S(1)} %copy-done.4, s32[8]{0:T(128)S(1)} %copy-done.5, s32[8]{0:T(128)S(1)} %copy-done.6, bf16[256,512]{1,0:T(8,128)(2,1)S(1)} %order.1.q0_ref, ...), custom_call_target="tpu_custom_call", output_to_operand_aliasing={{0}: (9, {}), {1}: (10, {}), {2}: (11, {})} | custom-call | flops 1073741824 | bytes 8388608 | tf_op jit(solution)/shard_map/step/pallas_call | solution.py:283
  62.1 5.1 %collective-permute-start.9 = (bf16[256,256]{1,0:T(8,128)(2,1)S(1)}, bf16[256,256]{1,0:T(8,128)(2,1)S(1)}, u32[]{:S(2)}, u32[]{:S(2)}) collective-permute-start(bf16[256,256]{1,0:T(8,128)(2,1)S(1)} %collective-permute-done.8.a_ref), channel_id=1, source_target_pairs={{0,8},{8,16},{16,24},{24,32},{32,40},{40,48},{48,56},{56,64},{64,7... | collective-permute-start | bytes 393224 | tf_op jit(solution)/shard_map/ppermute | solution.py:273
  67.3 1.7 %step.11 = (f32[4,4,128,256]{3,2,1,0:T(8,128)S(1)}, f32[4,4,8,256]{3,2,1,0:T(8,128)S(1)}, f32[4,4,8,256]{3,2,1,0:T(8,128)S(1)}) custom-call(s32[8]{0:T(128)S(1)} %copy-done.4, s32[8]{0:T(128)S(1)} %copy-done.5, s32[8]{0:T(128)S(1)} %copy-done.6, bf16[256,512]{1,0:T(8,128)(2,1)S(1)} %order.1.q0_ref, ...), custom_call_target="tpu_custom_call", output_to_operand_aliasing={{0}: (9, {}), {1}: (10, {}), {2}: (11, {})} | custom-call | flops 1073741824 | bytes 8388608 | tf_op jit(solution)/shard_map/step/pallas_call | solution.py:283
  69.0 1.9 %collective-permute-start.17 = (bf16[256,256]{1,0:T(8,128)(2,1)S(1)}, bf16[256,256]{1,0:T(8,128)(2,1)S(1)}, u32[]{:S(2)}, u32[]{:S(2)}) collective-permute-start(bf16[256,256]{1,0:T(8,128)(2,1)S(1)} %collective-permute-done.16.b_ref), channel_id=1, source_target_pairs={{0,120},{8,0},{16,8},{24,16},{32,24},{40,32},{48,40},{56,48},{64,5... | collective-permute-start | bytes 393224 | tf_op jit(solution)/shard_map/ppermute | solution.py:275
  71.8 5.1 %collective-permute-start.10 = (bf16[256,256]{1,0:T(8,128)(2,1)S(1)}, bf16[256,256]{1,0:T(8,128)(2,1)S(1)}, u32[]{:S(2)}, u32[]{:S(2)}) collective-permute-start(bf16[256,256]{1,0:T(8,128)(2,1)S(1)} %collective-permute-done.9.a_ref), channel_id=1, source_target_pairs={{0,8},{8,16},{16,24},{24,32},{32,40},{40,48},{48,56},{56,64},{64,7... | collective-permute-start | bytes 393224 | tf_op jit(solution)/shard_map/ppermute | solution.py:273
  78.0 4.3 %step.14 = (f32[4,4,128,256]{3,2,1,0:T(8,128)S(1)}, f32[4,4,8,256]{3,2,1,0:T(8,128)S(1)}, f32[4,4,8,256]{3,2,1,0:T(8,128)S(1)}) custom-call(s32[8]{0:T(128)S(1)} %copy-done.4, s32[8]{0:T(128)S(1)} %copy-done.5, s32[8]{0:T(128)S(1)} %copy-done.6, bf16[256,512]{1,0:T(8,128)(2,1)S(1)} %order.1.q0_ref, ...), custom_call_target="tpu_custom_call", output_to_operand_aliasing={{0}: (9, {}), {1}: (10, {}), {2}: (11, {})} | custom-call | flops 1073741824 | bytes 8388608 | tf_op jit(solution)/shard_map/step/pallas_call | solution.py:283
  83.6 39.7 %all_to_all.10.parts_ref = bf16[8,528,128]{2,1,0:T(8,128)(2,1)S(1)} all-to-all(bf16[8,528,128]{2,1,0:T(8,128)(2,1)S(1)} %finish.1), channel_id=1, replica_groups=mesh['y'=4,'z'=16,'x'=4,'core'=2] {'y','core'}, dimensions={0} | all-to-all | bytes 2162688 | tf_op jit(solution)/shard_map/all_to_all | solution.py:307
  123.3 2.8 %project.1 = bf16[128,4096]{1,0:T(8,128)(2,1)S(1)} custom-call(bf16[8,528,128]{2,1,0:T(8,128)(2,1)S(1)} %all_to_all.10.parts_ref, bf16[512,4096]{1,0:T(8,128)(2,1)S(1)} %copy-done, bf16[512,4096]{1,0:T(8,128)(2,1)S(1)} %collective-permute-done.18.other_w_ref), custom_call_target="tpu_custom_call" | custom-call | tf_op jit(solution)/shard_map/project/pallas_call | solution.py:310
  126.1 24.6 %all_to_all.11 = bf16[4,32,4096]{2,1,0:T(8,128)(2,1)S(1)} all-to-all(bf16[4,32,4096]{2,1,0:T(8,128)(2,1)S(1)} %bitcast.2), channel_id=1, replica_groups=mesh['y'=4,'z'=16,'x'=4,'core'=2] {'x'}, dimensions={0} | all-to-all | bytes 2097152 | tf_op jit(solution)/shard_map/all_to_all | solution.py:324
  (44 shorter events, 15.7 us)
Async XLA Ops:
  0.0 123.2 %collective-permute-start.18 = (bf16[512,4096]{1,0:T(8,128)(2,1)}, bf16[512,4096]{1,0:T(8,128)(2,1)S(1)}, u32[]{:S(2)}, u32[]{:S(2)}) collective-permute-start(bf16[512,4096]{1,0:T(8,128)(2,1)} %own_w_ref.1), channel_id=1, source_target_pairs={{0,1},{1,0},{2,3},{3,2},{4,5},{5,4},{6,7},{7,6},{8,9},{9,8},{10,11... | collective-permute-start | bytes 12582920 | tf_op jit(solution)/shard_map/ppermute | solution.py:280
  1.9 0.8 copy-start.2
  2.8 0.8 copy-start.3
  3.7 9.2 %collective-permute-start.3 = (bf16[256,256]{1,0:T(8,128)(2,1)S(1)}, bf16[256,256]{1,0:T(8,128)(2,1)S(1)}, u32[]{:S(2)}, u32[]{:S(2)}) collective-permute-start(bf16[256,256]{1,0:T(8,128)(2,1)S(1)} %pack.1.own_ref.b_ref), channel_id=1, source_target_pairs={{0,8},{8,16},{16,24},{24,32},{32,40},{40,48},{48,56},{56,64},{64,7... | collective-permute-start | bytes 393224 | tf_op jit(solution)/shard_map/ppermute | solution.py:273
  8.7 9.4 %collective-permute-start.11 = (bf16[256,256]{1,0:T(8,128)(2,1)S(1)}, bf16[256,256]{1,0:T(8,128)(2,1)S(1)}, u32[]{:S(2)}, u32[]{:S(2)}) collective-permute-start(bf16[256,256]{1,0:T(8,128)(2,1)S(1)} %pack.1.own_ref.b_ref), channel_id=1, source_target_pairs={{0,120},{8,0},{16,8},{24,16},{32,24},{40,32},{48,40},{56,48},{64,5... | collective-permute-start | bytes 393224 | tf_op jit(solution)/shard_map/ppermute | solution.py:275
  10.7 1.0 copy-start.1
  11.7 18.1 %collective-permute-start = (bf16[256,512]{1,0:T(8,128)(2,1)S(1)}, bf16[256,512]{1,0:T(8,128)(2,1)S(1)}, u32[]{:S(2)}, u32[]{:S(2)}) collective-permute-start(bf16[256,512]{1,0:T(8,128)(2,1)S(1)} %order.1.q0_ref), channel_id=1, source_target_pairs={{128,0},{256,128},{384,256},{129,1},{257,129},{385,257},{130,2},{2... | collective-permute-start | bytes 786440 | tf_op jit(solution)/shard_map/ppermute | solution.py:279
  13.0 8.0 %collective-permute-start.4 = (bf16[256,256]{1,0:T(8,128)(2,1)S(1)}, bf16[256,256]{1,0:T(8,128)(2,1)S(1)}, u32[]{:S(2)}, u32[]{:S(2)}) collective-permute-start(bf16[256,256]{1,0:T(8,128)(2,1)S(1)} %collective-permute-done.3.a_ref), channel_id=1, source_target_pairs={{0,8},{8,16},{16,24},{24,32},{32,40},{40,48},{48,56},{56,64},{64,7... | collective-permute-start | bytes 393224 | tf_op jit(solution)/shard_map/ppermute | solution.py:273
  18.1 8.4 %collective-permute-start.12 = (bf16[256,256]{1,0:T(8,128)(2,1)S(1)}, bf16[256,256]{1,0:T(8,128)(2,1)S(1)}, u32[]{:S(2)}, u32[]{:S(2)}) collective-permute-start(bf16[256,256]{1,0:T(8,128)(2,1)S(1)} %collective-permute-done.11.b_ref), channel_id=1, source_target_pairs={{0,120},{8,0},{16,8},{24,16},{32,24},{40,32},{48,40},{56,48},{64,5... | collective-permute-start | bytes 393224 | tf_op jit(solution)/shard_map/ppermute | solution.py:275
  20.9 10.1 %collective-permute-start.5 = (bf16[256,256]{1,0:T(8,128)(2,1)S(1)}, bf16[256,256]{1,0:T(8,128)(2,1)S(1)}, u32[]{:S(2)}, u32[]{:S(2)}) collective-permute-start(bf16[256,256]{1,0:T(8,128)(2,1)S(1)} %collective-permute-done.4.a_ref), channel_id=1, source_target_pairs={{0,8},{8,16},{16,24},{24,32},{32,40},{40,48},{48,56},{56,64},{64,7... | collective-permute-start | bytes 393224 | tf_op jit(solution)/shard_map/ppermute | solution.py:273
  26.5 9.7 %collective-permute-start.13 = (bf16[256,256]{1,0:T(8,128)(2,1)S(1)}, bf16[256,256]{1,0:T(8,128)(2,1)S(1)}, u32[]{:S(2)}, u32[]{:S(2)}) collective-permute-start(bf16[256,256]{1,0:T(8,128)(2,1)S(1)} %collective-permute-done.12.b_ref), channel_id=1, source_target_pairs={{0,120},{8,0},{16,8},{24,16},{32,24},{40,32},{48,40},{56,48},{64,5... | collective-permute-start | bytes 393224 | tf_op jit(solution)/shard_map/ppermute | solution.py:275
  28.5 21.3 %collective-permute-start.1 = (bf16[256,512]{1,0:T(8,128)(2,1)S(1)}, bf16[256,512]{1,0:T(8,128)(2,1)S(1)}, u32[]{:S(2)}, u32[]{:S(2)}) collective-permute-start(bf16[256,512]{1,0:T(8,128)(2,1)S(1)} %order.1.q0_ref), channel_id=1, source_target_pairs={{256,0},{384,128},{257,1},{385,129},{258,2},{386,130},{259,3},{387... | collective-permute-start | bytes 786440 | tf_op jit(solution)/shard_map/ppermute | solution.py:279
  29.8 20.0 %collective-permute-start.2 = (bf16[256,512]{1,0:T(8,128)(2,1)S(1)}, bf16[256,512]{1,0:T(8,128)(2,1)S(1)}, u32[]{:S(2)}, u32[]{:S(2)}) collective-permute-start(bf16[256,512]{1,0:T(8,128)(2,1)S(1)} %order.1.q0_ref), channel_id=1, source_target_pairs={{384,0},{385,1},{386,2},{387,3},{388,4},{389,5},{390,6},{391,7},{3... | collective-permute-start | bytes 786440 | tf_op jit(solution)/shard_map/ppermute | solution.py:279
  31.1 7.6 %collective-permute-start.6 = (bf16[256,256]{1,0:T(8,128)(2,1)S(1)}, bf16[256,256]{1,0:T(8,128)(2,1)S(1)}, u32[]{:S(2)}, u32[]{:S(2)}) collective-permute-start(bf16[256,256]{1,0:T(8,128)(2,1)S(1)} %collective-permute-done.5.a_ref), channel_id=1, source_target_pairs={{0,8},{8,16},{16,24},{24,32},{32,40},{40,48},{48,56},{56,64},{64,7... | collective-permute-start | bytes 393224 | tf_op jit(solution)/shard_map/ppermute | solution.py:273
  36.2 11.6 %collective-permute-start.14 = (bf16[256,256]{1,0:T(8,128)(2,1)S(1)}, bf16[256,256]{1,0:T(8,128)(2,1)S(1)}, u32[]{:S(2)}, u32[]{:S(2)}) collective-permute-start(bf16[256,256]{1,0:T(8,128)(2,1)S(1)} %collective-permute-done.13.b_ref), channel_id=1, source_target_pairs={{0,120},{8,0},{16,8},{24,16},{32,24},{40,32},{48,40},{56,48},{64,5... | collective-permute-start | bytes 393224 | tf_op jit(solution)/shard_map/ppermute | solution.py:275
  38.7 12.8 %collective-permute-start.7 = (bf16[256,256]{1,0:T(8,128)(2,1)S(1)}, bf16[256,256]{1,0:T(8,128)(2,1)S(1)}, u32[]{:S(2)}, u32[]{:S(2)}) collective-permute-start(bf16[256,256]{1,0:T(8,128)(2,1)S(1)} %collective-permute-done.6.a_ref), channel_id=1, source_target_pairs={{0,8},{8,16},{16,24},{24,32},{32,40},{40,48},{48,56},{56,64},{64,7... | collective-permute-start | bytes 393224 | tf_op jit(solution)/shard_map/ppermute | solution.py:273
  44.3 0.7 copy-start.4
  47.9 10.6 %collective-permute-start.15 = (bf16[256,256]{1,0:T(8,128)(2,1)S(1)}, bf16[256,256]{1,0:T(8,128)(2,1)S(1)}, u32[]{:S(2)}, u32[]{:S(2)}) collective-permute-start(bf16[256,256]{1,0:T(8,128)(2,1)S(1)} %collective-permute-done.14.b_ref), channel_id=1, source_target_pairs={{0,120},{8,0},{16,8},{24,16},{32,24},{40,32},{48,40},{56,48},{64,5... | collective-permute-start | bytes 393224 | tf_op jit(solution)/shard_map/ppermute | solution.py:275
  51.6 10.6 %collective-permute-start.8 = (bf16[256,256]{1,0:T(8,128)(2,1)S(1)}, bf16[256,256]{1,0:T(8,128)(2,1)S(1)}, u32[]{:S(2)}, u32[]{:S(2)}) collective-permute-start(bf16[256,256]{1,0:T(8,128)(2,1)S(1)} %collective-permute-done.7.a_ref), channel_id=1, source_target_pairs={{0,8},{8,16},{16,24},{24,32},{32,40},{40,48},{48,56},{56,64},{64,7... | collective-permute-start | bytes 393224 | tf_op jit(solution)/shard_map/ppermute | solution.py:273
  58.5 10.6 %collective-permute-start.16 = (bf16[256,256]{1,0:T(8,128)(2,1)S(1)}, bf16[256,256]{1,0:T(8,128)(2,1)S(1)}, u32[]{:S(2)}, u32[]{:S(2)}) collective-permute-start(bf16[256,256]{1,0:T(8,128)(2,1)S(1)} %collective-permute-done.15.b_ref), channel_id=1, source_target_pairs={{0,120},{8,0},{16,8},{24,16},{32,24},{40,32},{48,40},{56,48},{64,5... | collective-permute-start | bytes 393224 | tf_op jit(solution)/shard_map/ppermute | solution.py:275
  62.1 9.7 %collective-permute-start.9 = (bf16[256,256]{1,0:T(8,128)(2,1)S(1)}, bf16[256,256]{1,0:T(8,128)(2,1)S(1)}, u32[]{:S(2)}, u32[]{:S(2)}) collective-permute-start(bf16[256,256]{1,0:T(8,128)(2,1)S(1)} %collective-permute-done.8.a_ref), channel_id=1, source_target_pairs={{0,8},{8,16},{16,24},{24,32},{32,40},{40,48},{48,56},{56,64},{64,7... | collective-permute-start | bytes 393224 | tf_op jit(solution)/shard_map/ppermute | solution.py:273
  69.0 9.0 %collective-permute-start.17 = (bf16[256,256]{1,0:T(8,128)(2,1)S(1)}, bf16[256,256]{1,0:T(8,128)(2,1)S(1)}, u32[]{:S(2)}, u32[]{:S(2)}) collective-permute-start(bf16[256,256]{1,0:T(8,128)(2,1)S(1)} %collective-permute-done.16.b_ref), channel_id=1, source_target_pairs={{0,120},{8,0},{16,8},{24,16},{32,24},{40,32},{48,40},{56,48},{64,5... | collective-permute-start | bytes 393224 | tf_op jit(solution)/shard_map/ppermute | solution.py:275
  71.8 10.5 %collective-permute-start.10 = (bf16[256,256]{1,0:T(8,128)(2,1)S(1)}, bf16[256,256]{1,0:T(8,128)(2,1)S(1)}, u32[]{:S(2)}, u32[]{:S(2)}) collective-permute-start(bf16[256,256]{1,0:T(8,128)(2,1)S(1)} %collective-permute-done.9.a_ref), channel_id=1, source_target_pairs={{0,8},{8,16},{16,24},{24,32},{32,40},{40,48},{48,56},{56,64},{64,7... | collective-permute-start | bytes 393224 | tf_op jit(solution)/shard_map/ppermute | solution.py:273
  83.2 40.0 %copy-start = (bf16[512,4096]{1,0:T(8,128)(2,1)S(1)}, bf16[512,4096]{1,0:T(8,128)(2,1)}, u32[]{:S(2)}) copy-start(bf16[512,4096]{1,0:T(8,128)(2,1)} %own_w_ref.1) | copy-start | bytes 12582916
  (2 other events, 1.3 us)
where the time goes:
time: 152 us
  blocking collectives  64.3 us (42%)
  starting transfers between devices  61.1 us (40%)
  Pallas kernels  18.8 us (12%)
  local copies, waits for them, and re-layouts  4.58 us (3%)
    ppermute x8, starting transfers between devices, body(): a[d] = lax.ppermute(a[d - 1], 'z', ahead)  41.8 us
    all_to_all x1, blocking collectives, body(): parts = lax.all_to_all(packed, ('y', 'core'), 0, 0, tiled=True)  39.7 us
    all_to_all x1, blocking collectives, body(): pieces = lax.all_to_all(mixed.reshape(NX, 32, -1), 'x', 0, 0, tiled=True)  24.6 us
    pallas_call x8, Pallas kernels, body(): pl.pallas_call(functools.partial(step_kernel, d, d == half), out_shape=ST...  14 us
    ppermute x7, starting transfers between devices, body(): b[d] = lax.ppermute(b[d - 1], 'z', behind)  13.4 us
    unnamed x14, local copies, waits for them, and re-layouts  4.58 us
    ppermute x3, starting transfers between devices, body(): lax.ppermute(queries, 'y', [(i, i - k) for i in range(k, NY)])  3.88 us
  transfers between devices with their start and end apart: 19, of which 2 were waited for; matrix products, arithmetic and copies ran while one was open for 0% of the time, Pallas kernels for 11%

commit v1 on v0

--- a/solution.py
+++ b/solution.py
@@ -19,6 +19,7 @@
 MASKED = -3e30
 SCALE = 1.0 / math.sqrt(HD)
 EXP2_SCALE = SCALE * math.log2(math.e)
+LN2 = math.log(2.0)
 STAT_ROWS = 16
 PACK = GROUP * HD + STAT_ROWS
 NT = (((1,), (1,)), ((), ()))
@@ -45,7 +46,7 @@
 
 def fold(q_ref, slot, keys, values, mask, valid, acc, top, total):
     def score(h):
-        q = q_ref[slot, :, h * HD : (h + 1) * HD]
+        q = q_ref[slot, :, 2 * h * HD : 2 * (h + 1) * HD]
         out = []
         for k in keys:
             s = lax.dot_general(k, q, NT, preferred_element_type=jnp.float32)
@@ -69,14 +70,14 @@
             scores_next = score(h + 1)
             new_next = peaks(h + 1, scores_next)
         old = top[slot, h]
-        factor = jnp.exp2((old - new) * EXP2_SCALE)
+        factor = jnp.exp2(old - new)
         part = total[slot, h] * factor
         weights = []
         for n, s in enumerate(scores):
-            shift = new[:1] * EXP2_SCALE
+            shift = new[:1]
             if valid is not None:
                 shift = jnp.where(valid[n], shift, -MASKED)
-            w = jnp.exp2(s * EXP2_SCALE - shift)
+            w = jnp.exp2(s - shift)
             part = part + jnp.sum(w.reshape(ROWS // 8, 8, ROWS), axis=0)
             weights.append(w.astype(jnp.bfloat16))
         out = jnp.dot(
@@ -92,12 +93,13 @@
 
 
 def split_block(block_ref, k_ref, v_ref):
-    k_ref[...] = block_ref[:, :HD]
+    k_ref[:, :HD] = block_ref[:, :HD]
+    k_ref[:, HD:] = block_ref[:, :HD]
     v_ref[:, :HD] = block_ref[:HD, HD:]
     v_ref[:, HD:] = block_ref[HD:, HD:]
 
 
-def fold_masked(info, q_ref, slot, k_ref, v_ref, key_start, acc, top, total):
+def fold_masked(info, q_ref, slot, local, k_ref, v_ref, key_start, acc, top, total):
     kind, sink, window = info[2], info[3], info[4]
     query_start = (info[0] + slot) * ROW_KEYS + info[1] * ROWS
     needed = (key_start <= query_start + ROWS - 1) & (
@@ -109,74 +111,108 @@
         i = query_start + query_offsets((ROWS, ROWS))
         j = key_start + lax.broadcasted_iota(jnp.int32, (ROWS, ROWS), 0)
         mask = (j <= i) & ((kind == 1) | (j > i - window) | (j < sink))
-        fold(q_ref, slot, [k_ref[...]], [v_ref[...]], mask, None, acc, top, total)
-
-
-def first_kernel(kinds, sinks, windows, q_ref, own_ref, acc, top, total, k_ref, v_ref):
+        fold(q_ref, local, [k_ref[...]], [v_ref[...]], mask, None, acc, top, total)
+
+
+def scale_queries(q_ref, out_ref, local):
+    for h in range(GROUP):
+        scaled = q_ref[:, h * HD : (h + 1) * HD].astype(jnp.float32) * EXP2_SCALE
+        high = scaled.astype(jnp.bfloat16)
+        out_ref[local, :, 2 * h * HD : (2 * h + 1) * HD] = high
+        rest = scaled - high.astype(jnp.float32)
+        out_ref[local, :, (2 * h + 1) * HD : 2 * (h + 1) * HD] = rest.astype(jnp.bfloat16)
+
+
+def first_kernel(
+    kinds, sinks, windows, q_ref, own_ref, scaled, acc, top, total, acc1, top1, total1, k_ref, v_ref
+):
     info = read_info((kinds, sinks, windows))
-    acc[...] = jnp.zeros_like(acc)
-    top[...] = jnp.full_like(top, LOW)
-    total[...] = jnp.zeros_like(total)
+    for state in ((acc, top, total), (acc1, top1, total1)):
+        state[0][...] = jnp.zeros_like(state[0])
+        state[1][...] = jnp.full_like(state[1], LOW)
+        state[2][...] = jnp.zeros_like(state[2])
+    scale_queries(q_ref, scaled, 0)
     own_start = info[0] * ROW_KEYS + info[1] * ROWS
     split_block(own_ref, k_ref, v_ref)
-    fold_masked(info, q_ref, 0, k_ref, v_ref, own_start, acc, top, total)
+    fold_masked(info, scaled, 0, 0, k_ref, v_ref, own_start, acc, top, total)
+
+
+def join_kernel(scaled_ref, q1_ref, out_ref):
+    out_ref[0] = scaled_ref[0]
+    scale_queries(q1_ref, out_ref, 1)
+
+
+def pair_kernel(q2_ref, q3_ref, out_ref):
+    scale_queries(q2_ref, out_ref, 0)
+    scale_queries(q3_ref, out_ref, 1)
 
 
 def step_kernel(
-    distance, last, kinds, sinks, windows, q0_ref, q1_ref, q2_ref, q3_ref, a_ref, b_ref,
-    acc_in, top_in, total_in, acc, top, total, q_ref, k_ref, v_ref
+    distance, last, part, kinds, sinks, windows, q_ref, a_ref, b_ref,
+    acc_in, top_in, total_in, acc, top, total, k_ref, v_ref
 ):
     del acc_in, top_in, total_in
     info = read_info((kinds, sinks, windows))
     y, z, kind = info[0], info[1], info[2]
-    slots = NY - y
+    base = 2 * part
+    count = jnp.clip(NY - y - base, 0, 2)
     a_place = lax.rem(z - distance + NZ, NZ)
     b_place = lax.rem(z + (0 if last else distance), NZ)
-    q_ref[0] = q0_ref[...]
-    q_ref[1] = q1_ref[...]
-    q_ref[2] = q2_ref[...]
-    q_ref[3] = q3_ref[...]
-    split_block(a_ref, k_ref.at[0], v_ref.at[0])
-    split_block(b_ref, k_ref.at[1], v_ref.at[1])
     a_before = a_place < z
     b_before = b_place < z
 
+    @pl.when(count > 0)
+    def _():
+        split_block(a_ref, k_ref.at[0], v_ref.at[0])
+        split_block(b_ref, k_ref.at[1], v_ref.at[1])
+
     @pl.when(kind == 1)
     def _():
-        @pl.loop(jnp.where(a_before | b_before, 0, 1), slots)
-        def _(slot):
-            valid = [(slot > 0) | a_before, (slot > 0) | b_before]
-            fold(q_ref, slot, [k_ref[0], k_ref[1]], [v_ref[0], v_ref[1]], None, valid, acc, top, total)
+        first = 0 if part else jnp.where(a_before | b_before, 0, 1)
+
+        @pl.loop(first, count)
+        def _(n):
+            valid = None if part else [(n > 0) | a_before, (n > 0) | b_before]
+            fold(q_ref, n, [k_ref[0], k_ref[1]], [v_ref[0], v_ref[1]], None, valid, acc, top, total)
 
     @pl.when(kind != 1)
     def _():
-        @pl.loop(0, 2 * slots)
+        @pl.loop(0, 2 * count)
         def _(n):
-            slot = n // 2
+            local = n // 2
             side = n % 2
+            slot = base + local
             place = jnp.where(side == 0, a_place, b_place)
             skip = (slot == 0) & (place == z)
 
             @pl.when(jnp.logical_not(skip))
             def _():
                 key_start = y * ROW_KEYS + place * ROWS
-                fold_masked(info, q_ref, slot, k_ref.at[side], v_ref.at[side], key_start, acc, top, total)
-
-
-def finish_kernel(acc, top, total, out_ref):
+                fold_masked(
+                    info, q_ref, slot, local, k_ref.at[side], v_ref.at[side], key_start, acc, top, total
+                )
+
+
+def finish_kernel(acc0, top0, total0, acc1, top1, total1, out_ref):
     y = lax.axis_index("y")
-    for target in range(NY):
-        slot = jnp.maximum(target - y, 0)
-        valid = target >= y
+
+    @pl.loop(0, y * NC)
+    def _(piece):
+        out_ref[piece, : GROUP * HD] = jnp.zeros((GROUP * HD, 128), jnp.bfloat16)
+        out_ref[piece, GROUP * HD :] = jnp.full((STAT_ROWS, 128), LOW, jnp.bfloat16)
+
+    def send(slot):
+        local = slot % 2
+        acc, top, total = ((acc0, top0, total0), (acc1, top1, total1))[slot // 2]
         parts = []
         for h in range(GROUP):
-            s = jnp.sum(total[slot, h], axis=0, keepdims=True)
-            have = (s > 0.0) & valid
+            s = jnp.sum(total[local, h], axis=0, keepdims=True)
+            have = s > 0.0
             safe = jnp.where(have, s, 1.0)
-            o = jnp.where(have, acc[slot, h] * (1.0 / safe), 0.0).astype(jnp.bfloat16)
-            lse = jnp.where(have, top[slot, h][:1] * SCALE + jnp.log(safe), LOW)
+            o = (acc[local, h] * (1.0 / safe)).astype(jnp.bfloat16)
+            lse = jnp.where(have, top[local, h][:1] * LN2 + jnp.log(safe), LOW)
             for c in range(NC):
-                out_ref[target * NC + c, h * HD : (h + 1) * HD, :] = o[:, c * 128 : (c + 1) * 128]
+                out_ref[(y + slot) * NC + c, h * HD : (h + 1) * HD, :] = o[:, c * 128 : (c + 1) * 128]
             high = lse.astype(jnp.bfloat16).astype(jnp.float32)
             rest = lse - high
             mid = rest.astype(jnp.bfloat16).astype(jnp.float32)
@@ -184,7 +220,11 @@
         parts += [jnp.zeros_like(parts[0])] * (STAT_ROWS - len(parts))
         packed = jnp.concatenate(parts, axis=0).astype(jnp.bfloat16)
         for c in range(NC):
-            out_ref[target * NC + c, GROUP * HD :, :] = packed[:, c * 128 : (c + 1) * 128]
+            out_ref[(y + slot) * NC + c, GROUP * HD :, :] = packed[:, c * 128 : (c + 1) * 128]
+
+    send(0)
+    for slot in range(1, NY):
+        pl.when(slot < NY - y)(functools.partial(send, slot))
 
 
 def project_kernel(parts_ref, own_w_ref, other_w_ref, out_ref, mix):
@@ -224,9 +264,9 @@
 VMEM_SPEC = pl.BlockSpec(memory_space=pltpu.VMEM)
 SMEM_SPEC = pl.BlockSpec(memory_space=pltpu.SMEM)
 STATE = [
-    jax.ShapeDtypeStruct((NY, GROUP, HD, ROWS), jnp.float32),
-    jax.ShapeDtypeStruct((NY, GROUP, 8, ROWS), jnp.float32),
-    jax.ShapeDtypeStruct((NY, GROUP, 8, ROWS), jnp.float32),
+    jax.ShapeDtypeStruct((2, GROUP, HD, ROWS), jnp.float32),
+    jax.ShapeDtypeStruct((2, GROUP, 8, ROWS), jnp.float32),
+    jax.ShapeDtypeStruct((2, GROUP, 8, ROWS), jnp.float32),
 ]
 
 
@@ -238,16 +278,18 @@
     heads = (head_kind, sink_len, window_len)
     own = pl.pallas_call(
         pack_kernel,
+        grid=(1,),
         out_shape=jax.ShapeDtypeStruct((ROWS, 2 * HD), jnp.bfloat16),
-        in_specs=[VMEM_SPEC] * 2,
+        in_specs=[pl.BlockSpec((ROWS, HD), lambda i: (0, 0))] * 2,
         out_specs=VMEM_SPEC,
         compiler_params=params(),
         name="pack",
     )(keys, values)
     queries = pl.pallas_call(
         order_kernel,
+        grid=(1,),
         out_shape=jax.ShapeDtypeStruct(queries.shape, jnp.bfloat16),
-        in_specs=[VMEM_SPEC],
+        in_specs=[pl.BlockSpec(queries.shape, lambda i: (0, 0))],
         out_specs=VMEM_SPEC,
         compiler_params=params(),
         name="order",
@@ -258,16 +300,21 @@
     half = NZ // 2
     a, b = {0: own}, {0: own}
     cost = pl.CostEstimate(flops=1 << 30, bytes_accessed=8 << 20, transcendentals=1 << 22)
-    state = pl.pallas_call(
+    scaled_type = jax.ShapeDtypeStruct((2, ROWS, 2 * GROUP * HD), jnp.bfloat16)
+    scaled, *state = pl.pallas_call(
         first_kernel,
-        out_shape=STATE,
+        out_shape=[scaled_type] + STATE * 2,
         in_specs=[SMEM_SPEC] * 3 + [VMEM_SPEC] * 2,
-        out_specs=[VMEM_SPEC] * 3,
-        scratch_shapes=[pltpu.VMEM((ROWS, HD), jnp.bfloat16), pltpu.VMEM((HD, ROWS), jnp.bfloat16)],
+        out_specs=[VMEM_SPEC] * 7,
+        scratch_shapes=[
+            pltpu.VMEM((ROWS, 2 * HD), jnp.bfloat16),
+            pltpu.VMEM((HD, ROWS), jnp.bfloat16),
+        ],
         compiler_params=params(),
         cost_estimate=cost,
         name="first",
-    )(*heads, queries[None], own)
+    )(*heads, queries, own)
+    states = [state[:3], state[3:]]
 
     for d in range(1, half + 1):
         a[d] = lax.ppermute(a[d - 1], "z", ahead)
@@ -279,31 +326,41 @@
         received.append(lax.ppermute(queries, "y", [(i, i - k) for i in range(k, NY)]))
     other_w = lax.ppermute(w_out, "core", [(0, 1), (1, 0)])
 
+    slots = [
+        pl.pallas_call(
+            kernel,
+            out_shape=scaled_type,
+            in_specs=[VMEM_SPEC] * 2,
+            out_specs=VMEM_SPEC,
+            compiler_params=params(),
+        )(*operands)
+        for kernel, operands in ((join_kernel, (scaled, received[0])), (pair_kernel, received[1:]))
+    ]
     for d in range(1, half + 1):
-        state = pl.pallas_call(
-            functools.partial(step_kernel, d, d == half),
-            out_shape=STATE,
-            in_specs=[SMEM_SPEC] * 3 + [VMEM_SPEC] * 9,
-            out_specs=[VMEM_SPEC] * 3,
-            scratch_shapes=[
-                pltpu.VMEM((NY, ROWS, GROUP * HD), jnp.bfloat16),
-                pltpu.VMEM((2, ROWS, HD), jnp.bfloat16),
-                pltpu.VMEM((2, HD, ROWS), jnp.bfloat16),
-            ],
-            input_output_aliases={9: 0, 10: 1, 11: 2},
-            compiler_params=params(),
-            cost_estimate=cost,
-            name="step",
-        )(*heads, queries, *received, a[d], b[d], *state)
+        for part in range(2):
+            states[part] = pl.pallas_call(
+                functools.partial(step_kernel, d, d == half, part),
+                out_shape=STATE,
+                in_specs=[SMEM_SPEC] * 3 + [VMEM_SPEC] * 6,
+                out_specs=[VMEM_SPEC] * 3,
+                scratch_shapes=[
+                    pltpu.VMEM((2, ROWS, 2 * HD), jnp.bfloat16),
+                    pltpu.VMEM((2, HD, ROWS), jnp.bfloat16),
+                ],
+                input_output_aliases={6: 0, 7: 1, 8: 2},
+                compiler_params=params(),
+                cost_estimate=cost,
+                name="step",
+            )(*heads, slots[part], a[d], b[d], *states[part])
 
     packed = pl.pallas_call(
         finish_kernel,
         out_shape=jax.ShapeDtypeStruct((NY * NC, PACK, ROWS // NC), jnp.bfloat16),
-        in_specs=[VMEM_SPEC] * 3,
+        in_specs=[VMEM_SPEC] * 6,
         out_specs=VMEM_SPEC,
         compiler_params=params(),
         name="finish",
-    )(*state)
+    )(*states[0], *states[1])
     parts = lax.all_to_all(packed, ("y", "core"), 0, 0, tiled=True)
 
     width = 1024

time: 152 us -> 155 us (1.020)
  starting transfers between devices: 61.1 us -> 57 us
  Pallas kernels: 18.8 us -> 22.9 us
  waiting for transfers between devices: 1.5 us -> 4.25 us
    ppermute x8, starting transfers between devices: 41.8 us -> 34.9 us  [body(): a[d] = lax.ppermute(a[d - 1], 'z', ahead)]
    pallas_call x11 -> x21, Pallas kernels: 15.7 us -> 19.8 us  [the longest x16 17.7 us: body(): pl.pallas_call(functools.partial(step_kernel, d, d == half, part), out_sh...]
    ppermute x7, waiting for transfers between devices: 0.02 us -> 4.06 us  [body(): b[d] = lax.ppermute(b[d - 1], 'z', behind)]
    ppermute x7, starting transfers between devices: 13.4 us -> 16.2 us  [body(): b[d] = lax.ppermute(b[d - 1], 'z', behind)]
  transfers between devices with their start and end apart: 19 -> 19, of which waited for: 2 -> 2; matrix products, arithmetic and copies ran while one was open for 0% -> 0% of each run, Pallas kernels for 11% -> 13%
where the time goes in v1:
time: 155 us; the launch traced here: 154 us
  blocking collectives  63.8 us (41%)
  starting transfers between devices  57 us (37%)
  Pallas kernels  22.9 us (15%)
  local copies, waits for them, and re-layouts  4.58 us (3%)
  waiting for transfers between devices  4.25 us (3%)
    all_to_all x1, blocking collectives, body(): parts = lax.all_to_all(packed, ('y', 'core'), 0, 0, tiled=True)  39.4 us
    ppermute x8, starting transfers between devices, body(): a[d] = lax.ppermute(a[d - 1], 'z', ahead)  34.9 us
    all_to_all x1, blocking collectives, body(): pieces = lax.all_to_all(mixed.reshape(NX, 32, -1), 'x', 0, 0, tiled=True)  24.4 us
    pallas_call x16, Pallas kernels, body(): pl.pallas_call(functools.partial(step_kernel, d, d == half, part), out_sh...  17.7 us
    ppermute x7, starting transfers between devices, body(): b[d] = lax.ppermute(b[d - 1], 'z', behind)  16.2 us
    unnamed x14, local copies, waits for them, and re-layouts  4.58 us
    ppermute x7, waiting for transfers between devices, body(): b[d] = lax.ppermute(b[d - 1], 'z', behind)  4.06 us
    ppermute x3, starting transfers between devices, body(): lax.ppermute(queries, 'y', [(i, i - k) for i in range(k, NY)])  3.86 us
  transfers between devices with their start and end apart: 19, of which 2 were waited for; matrix products, arithmetic and copies ran while one was open for 0% of the time, Pallas kernels for 13%

profile of v1, /device:TPU:224, one launch (start us, length us, event | category | flops | bytes accessed | tf_op | source)
XLA Modules:
  0.0 153.9 jit_solution(4376247567215369195)
XLA Ops:
  0.0 1.9 %collective-permute-start.18 = (bf16[512,4096]{1,0:T(8,128)(2,1)}, bf16[512,4096]{1,0:T(8,128)(2,1)S(1)}, u32[]{:S(2)}, u32[]{:S(2)}) collective-permute-start(bf16[512,4096]{1,0:T(8,128)(2,1)} %own_w_ref.1), channel_id=1, source_target_pairs={{0,1},{1,0},{2,3},{3,2},{4,5},{5,4},{6,7},{7,6},{8,9},{9,8},{10,11... | collective-permute-start | bytes 12582920 | tf_op jit(solution)/shard_map/ppermute | solution.py:327
  6.0 5.0 %collective-permute-start.1 = (bf16[256,256]{1,0:T(8,128)(2,1)S(1)}, bf16[256,256]{1,0:T(8,128)(2,1)S(1)}, u32[]{:S(2)}, u32[]{:S(2)}) collective-permute-start(bf16[256,256]{1,0:T(8,128)(2,1)S(1)} %pack.1.own_ref.b_ref), channel_id=1, source_target_pairs={{0,8},{8,16},{16,24},{24,32},{32,40},{40,48},{48,56},{56,64},{64,7... | collective-permute-start | bytes 393224 | tf_op jit(solution)/shard_map/ppermute | solution.py:320
  11.0 1.9 %collective-permute-start.9 = (bf16[256,256]{1,0:T(8,128)(2,1)S(1)}, bf16[256,256]{1,0:T(8,128)(2,1)S(1)}, u32[]{:S(2)}, u32[]{:S(2)}) collective-permute-start(bf16[256,256]{1,0:T(8,128)(2,1)S(1)} %pack.1.own_ref.b_ref), channel_id=1, source_target_pairs={{0,120},{8,0},{16,8},{24,16},{32,24},{40,32},{48,40},{56,48},{64,5... | collective-permute-start | bytes 393224 | tf_op jit(solution)/shard_map/ppermute | solution.py:322
  15.7 4.0 %collective-permute-done.9.b_ref = bf16[256,256]{1,0:T(8,128)(2,1)S(1)} collective-permute-done((bf16[256,256]{1,0:T(8,128)(2,1)S(1)}, bf16[256,256]{1,0:T(8,128)(2,1)S(1)}, u32[]{:S(2)}, u32[]{:S(2)}) %collective-permute-start.9) | collective-permute-done | bytes 131104 | tf_op jit(solution)/shard_map/ppermute | solution.py:322
  19.7 1.9 %collective-permute-start.2 = (bf16[256,256]{1,0:T(8,128)(2,1)S(1)}, bf16[256,256]{1,0:T(8,128)(2,1)S(1)}, u32[]{:S(2)}, u32[]{:S(2)}) collective-permute-start(bf16[256,256]{1,0:T(8,128)(2,1)S(1)} %collective-permute-done.1.a_ref), channel_id=1, source_target_pairs={{0,8},{8,16},{16,24},{24,32},{32,40},{40,48},{48,56},{56,64},{64,7... | collective-permute-start | bytes 393224 | tf_op jit(solution)/shard_map/ppermute | solution.py:320
  21.7 3.9 %collective-permute-start.10 = (bf16[256,256]{1,0:T(8,128)(2,1)S(1)}, bf16[256,256]{1,0:T(8,128)(2,1)S(1)}, u32[]{:S(2)}, u32[]{:S(2)}) collective-permute-start(bf16[256,256]{1,0:T(8,128)(2,1)S(1)} %collective-permute-done.9.b_ref), channel_id=1, source_target_pairs={{0,120},{8,0},{16,8},{24,16},{32,24},{40,32},{48,40},{56,48},{64,5... | collective-permute-start | bytes 393224 | tf_op jit(solution)/shard_map/ppermute | solution.py:322
  27.6 1.6 %first.1 = (bf16[2,256,1024]{2,1,0:T(8,128)(2,1)S(1)}, f32[2,4,128,256]{3,2,1,0:T(8,128)S(1)}, f32[2,4,8,256]{3,2,1,0:T(8,128)S(1)}, f32[2,4,8,256]{3,2,1,0:T(8,...) custom-call(s32[8]{0:T(128)S(1)} %copy-done.4, ...), custom_call_target="tpu_custom_call" | custom-call | flops 1073741824 | bytes 8388608 | tf_op jit(solution)/shard_map/first/pallas_call | solution.py:304
  29.2 3.1 %collective-permute-start.3 = (bf16[256,256]{1,0:T(8,128)(2,1)S(1)}, bf16[256,256]{1,0:T(8,128)(2,1)S(1)}, u32[]{:S(2)}, u32[]{:S(2)}) collective-permute-start(bf16[256,256]{1,0:T(8,128)(2,1)S(1)} %collective-permute-done.2.a_ref), channel_id=1, source_target_pairs={{0,8},{8,16},{16,24},{24,32},{32,40},{40,48},{48,56},{56,64},{64,7... | collective-permute-start | bytes 393224 | tf_op jit(solution)/shard_map/ppermute | solution.py:320
  32.3 2.7 %collective-permute-start.11 = (bf16[256,256]{1,0:T(8,128)(2,1)S(1)}, bf16[256,256]{1,0:T(8,128)(2,1)S(1)}, u32[]{:S(2)}, u32[]{:S(2)}) collective-permute-start(bf16[256,256]{1,0:T(8,128)(2,1)S(1)} %collective-permute-done.10.b_ref), channel_id=1, source_target_pairs={{0,120},{8,0},{16,8},{24,16},{32,24},{40,32},{48,40},{56,48},{64,5... | collective-permute-start | bytes 393224 | tf_op jit(solution)/shard_map/ppermute | solution.py:322
  39.9 4.3 %collective-permute-start.4 = (bf16[256,256]{1,0:T(8,128)(2,1)S(1)}, bf16[256,256]{1,0:T(8,128)(2,1)S(1)}, u32[]{:S(2)}, u32[]{:S(2)}) collective-permute-start(bf16[256,256]{1,0:T(8,128)(2,1)S(1)} %collective-permute-done.3.a_ref), channel_id=1, source_target_pairs={{0,8},{8,16},{16,24},{24,32},{32,40},{40,48},{48,56},{56,64},{64,7... | collective-permute-start | bytes 393224 | tf_op jit(solution)/shard_map/ppermute | solution.py:320
  44.3 1.9 %collective-permute-start.12 = (bf16[256,256]{1,0:T(8,128)(2,1)S(1)}, bf16[256,256]{1,0:T(8,128)(2,1)S(1)}, u32[]{:S(2)}, u32[]{:S(2)}) collective-permute-start(bf16[256,256]{1,0:T(8,128)(2,1)S(1)} %collective-permute-done.11.b_ref), channel_id=1, source_target_pairs={{0,120},{8,0},{16,8},{24,16},{32,24},{40,32},{48,40},{56,48},{64,5... | collective-permute-start | bytes 393224 | tf_op jit(solution)/shard_map/ppermute | solution.py:322
  48.4 5.1 %collective-permute-start.5 = (bf16[256,256]{1,0:T(8,128)(2,1)S(1)}, bf16[256,256]{1,0:T(8,128)(2,1)S(1)}, u32[]{:S(2)}, u32[]{:S(2)}) collective-permute-start(bf16[256,256]{1,0:T(8,128)(2,1)S(1)} %collective-permute-done.4.a_ref), channel_id=1, source_target_pairs={{0,8},{8,16},{16,24},{24,32},{32,40},{40,48},{48,56},{56,64},{64,7... | collective-permute-start | bytes 393224 | tf_op jit(solution)/shard_map/ppermute | solution.py:320
  53.5 1.9 %collective-permute-start.13 = (bf16[256,256]{1,0:T(8,128)(2,1)S(1)}, bf16[256,256]{1,0:T(8,128)(2,1)S(1)}, u32[]{:S(2)}, u32[]{:S(2)}) collective-permute-start(bf16[256,256]{1,0:T(8,128)(2,1)S(1)} %collective-permute-done.12.b_ref), channel_id=1, source_target_pairs={{0,120},{8,0},{16,8},{24,16},{32,24},{40,32},{48,40},{56,48},{64,5... | collective-permute-start | bytes 393224 | tf_op jit(solution)/shard_map/ppermute | solution.py:322
  55.5 1.6 %step.19 = (f32[2,4,128,256]{3,2,1,0:T(8,128)S(1)}, f32[2,4,8,256]{3,2,1,0:T(8,128)S(1)}, f32[2,4,8,256]{3,2,1,0:T(8,128)S(1)}) custom-call(s32[8]{0:T(128)S(1)} %copy-done.4, s32[8]{0:T(128)S(1)} %copy-done.5, s32[8]{0:T(128)S(1)} %copy-done.6, ...), custom_call_target="tpu_custom_call", output_to_operand_aliasing={{0}: (6, {}), {1}: (7, {}), {2}: (8, {})} | custom-call | flops 1073741824 | bytes 8388608 | tf_op jit(solution)/shard_map/step/pallas_call | solution.py:341
  57.8 5.1 %collective-permute-start.6 = (bf16[256,256]{1,0:T(8,128)(2,1)S(1)}, bf16[256,256]{1,0:T(8,128)(2,1)S(1)}, u32[]{:S(2)}, u32[]{:S(2)}) collective-permute-start(bf16[256,256]{1,0:T(8,128)(2,1)S(1)} %collective-permute-done.5.a_ref), channel_id=1, source_target_pairs={{0,8},{8,16},{16,24},{24,32},{32,40},{40,48},{48,56},{56,64},{64,7... | collective-permute-start | bytes 393224 | tf_op jit(solution)/shard_map/ppermute | solution.py:320
  63.0 1.9 %collective-permute-start.14 = (bf16[256,256]{1,0:T(8,128)(2,1)S(1)}, bf16[256,256]{1,0:T(8,128)(2,1)S(1)}, u32[]{:S(2)}, u32[]{:S(2)}) collective-permute-start(bf16[256,256]{1,0:T(8,128)(2,1)S(1)} %collective-permute-done.13.b_ref), channel_id=1, source_target_pairs={{0,120},{8,0},{16,8},{24,16},{32,24},{40,32},{48,40},{56,48},{64,5... | collective-permute-start | bytes 393224 | tf_op jit(solution)/shard_map/ppermute | solution.py:322
  66.4 5.1 %collective-permute-start.7 = (bf16[256,256]{1,0:T(8,128)(2,1)S(1)}, bf16[256,256]{1,0:T(8,128)(2,1)S(1)}, u32[]{:S(2)}, u32[]{:S(2)}) collective-permute-start(bf16[256,256]{1,0:T(8,128)(2,1)S(1)} %collective-permute-done.6.a_ref), channel_id=1, source_target_pairs={{0,8},{8,16},{16,24},{24,32},{32,40},{40,48},{48,56},{56,64},{64,7... | collective-permute-start | bytes 393224 | tf_op jit(solution)/shard_map/ppermute | solution.py:320
  71.6 1.9 %collective-permute-start.15 = (bf16[256,256]{1,0:T(8,128)(2,1)S(1)}, bf16[256,256]{1,0:T(8,128)(2,1)S(1)}, u32[]{:S(2)}, u32[]{:S(2)}) collective-permute-start(bf16[256,256]{1,0:T(8,128)(2,1)S(1)} %collective-permute-done.14.b_ref), channel_id=1, source_target_pairs={{0,120},{8,0},{16,8},{24,16},{32,24},{40,32},{48,40},{56,48},{64,5... | collective-permute-start | bytes 393224 | tf_op jit(solution)/shard_map/ppermute | solution.py:322
  75.0 5.1 %collective-permute-start.8 = (bf16[256,256]{1,0:T(8,128)(2,1)S(1)}, bf16[256,256]{1,0:T(8,128)(2,1)S(1)}, u32[]{:S(2)}, u32[]{:S(2)}) collective-permute-start(bf16[256,256]{1,0:T(8,128)(2,1)S(1)} %collective-permute-done.7.a_ref), channel_id=1, source_target_pairs={{0,8},{8,16},{16,24},{24,32},{32,40},{40,48},{48,56},{56,64},{64,7... | collective-permute-start | bytes 393224 | tf_op jit(solution)/shard_map/ppermute | solution.py:320
  80.1 2.1 %step.22 = (f32[2,4,128,256]{3,2,1,0:T(8,128)S(1)}, f32[2,4,8,256]{3,2,1,0:T(8,128)S(1)}, f32[2,4,8,256]{3,2,1,0:T(8,128)S(1)}) custom-call(s32[8]{0:T(128)S(1)} %copy-done.4, s32[8]{0:T(128)S(1)} %copy-done.5, s32[8]{0:T(128)S(1)} %copy-done.6, ...), custom_call_target="tpu_custom_call", output_to_operand_aliasing={{0}: (6, {}), {1}: (7, {}), {2}: (8, {})} | custom-call | flops 1073741824 | bytes 8388608 | tf_op jit(solution)/shard_map/step/pallas_call | solution.py:341
  82.3 2.3 %step.30 = (f32[2,4,128,256]{3,2,1,0:T(8,128)S(1)}, f32[2,4,8,256]{3,2,1,0:T(8,128)S(1)}, f32[2,4,8,256]{3,2,1,0:T(8,128)S(1)}) custom-call(s32[8]{0:T(128)S(1)} %copy-done.4, s32[8]{0:T(128)S(1)} %copy-done.5, s32[8]{0:T(128)S(1)} %copy-done.6, ...), custom_call_target="tpu_custom_call", output_to_operand_aliasing={{0}: (6, {}), {1}: (7, {}), {2}: (8, {})} | custom-call | flops 1073741824 | bytes 8388608 | tf_op jit(solution)/shard_map/step/pallas_call | solution.py:341
  86.4 39.4 %all_to_all.10.parts_ref = bf16[8,528,128]{2,1,0:T(8,128)(2,1)S(1)} all-to-all(bf16[8,528,128]{2,1,0:T(8,128)(2,1)S(1)} %finish.1), channel_id=1, replica_groups=mesh['y'=4,'z'=16,'x'=4,'core'=2] {'y','core'}, dimensions={0} | all-to-all | bytes 2162688 | tf_op jit(solution)/shard_map/all_to_all | solution.py:364
  125.8 2.8 %project.1 = bf16[128,4096]{1,0:T(8,128)(2,1)S(1)} custom-call(bf16[8,528,128]{2,1,0:T(8,128)(2,1)S(1)} %all_to_all.10.parts_ref, bf16[512,4096]{1,0:T(8,128)(2,1)S(1)} %copy-done, bf16[512,4096]{1,0:T(8,128)(2,1)S(1)} %collective-permute-done.18.other_w_ref), custom_call_target="tpu_custom_call" | custom-call | tf_op jit(solution)/shard_map/project/pallas_call | solution.py:367
  128.7 24.4 %all_to_all.11 = bf16[4,32,4096]{2,1,0:T(8,128)(2,1)S(1)} all-to-all(bf16[4,32,4096]{2,1,0:T(8,128)(2,1)S(1)} %bitcast.1), channel_id=1, replica_groups=mesh['y'=4,'z'=16,'x'=4,'core'=2] {'x'}, dimensions={0} | all-to-all | bytes 2097152 | tf_op jit(solution)/shard_map/all_to_all | solution.py:381
  (54 shorter events, 22.1 us)
Async XLA Ops:
  0.0 125.8 %collective-permute-start.18 = (bf16[512,4096]{1,0:T(8,128)(2,1)}, bf16[512,4096]{1,0:T(8,128)(2,1)S(1)}, u32[]{:S(2)}, u32[]{:S(2)}) collective-permute-start(bf16[512,4096]{1,0:T(8,128)(2,1)} %own_w_ref.1), channel_id=1, source_target_pairs={{0,1},{1,0},{2,3},{3,2},{4,5},{5,4},{6,7},{7,6},{8,9},{9,8},{10,11... | collective-permute-start | bytes 12582920 | tf_op jit(solution)/shard_map/ppermute | solution.py:327
  1.9 1.0 copy-start.1
  2.9 18.8 %collective-permute-start = (bf16[256,512]{1,0:T(8,128)(2,1)S(1)}, bf16[256,512]{1,0:T(8,128)(2,1)S(1)}, u32[]{:S(2)}, u32[]{:S(2)}) collective-permute-start(bf16[256,512]{1,0:T(8,128)(2,1)S(1)} %order.1.q_ref), channel_id=1, source_target_pairs={{128,0},{256,128},{384,256},{129,1},{257,129},{385,257},{130,2},{2... | collective-permute-start | bytes 786440 | tf_op jit(solution)/shard_map/ppermute | solution.py:326
  4.2 0.8 copy-start.2
  5.0 0.8 copy-start.3
  6.0 8.4 %collective-permute-start.1 = (bf16[256,256]{1,0:T(8,128)(2,1)S(1)}, bf16[256,256]{1,0:T(8,128)(2,1)S(1)}, u32[]{:S(2)}, u32[]{:S(2)}) collective-permute-start(bf16[256,256]{1,0:T(8,128)(2,1)S(1)} %pack.1.own_ref.b_ref), channel_id=1, source_target_pairs={{0,8},{8,16},{16,24},{24,32},{32,40},{40,48},{48,56},{56,64},{64,7... | collective-permute-start | bytes 393224 | tf_op jit(solution)/shard_map/ppermute | solution.py:320
  11.0 8.7 %collective-permute-start.9 = (bf16[256,256]{1,0:T(8,128)(2,1)S(1)}, bf16[256,256]{1,0:T(8,128)(2,1)S(1)}, u32[]{:S(2)}, u32[]{:S(2)}) collective-permute-start(bf16[256,256]{1,0:T(8,128)(2,1)S(1)} %pack.1.own_ref.b_ref), channel_id=1, source_target_pairs={{0,120},{8,0},{16,8},{24,16},{32,24},{40,32},{48,40},{56,48},{64,5... | collective-permute-start | bytes 393224 | tf_op jit(solution)/shard_map/ppermute | solution.py:322
  13.0 22.3 %collective-permute-start.16 = (bf16[256,512]{1,0:T(8,128)(2,1)S(1)}, bf16[256,512]{1,0:T(8,128)(2,1)S(1)}, u32[]{:S(2)}, u32[]{:S(2)}) collective-permute-start(bf16[256,512]{1,0:T(8,128)(2,1)S(1)} %order.1.q_ref), channel_id=1, source_target_pairs={{256,0},{384,128},{257,1},{385,129},{258,2},{386,130},{259,3},{387... | collective-permute-start | bytes 786440 | tf_op jit(solution)/shard_map/ppermute | solution.py:326
  14.4 20.8 %collective-permute-start.17 = (bf16[256,512]{1,0:T(8,128)(2,1)S(1)}, bf16[256,512]{1,0:T(8,128)(2,1)S(1)}, u32[]{:S(2)}, u32[]{:S(2)}) collective-permute-start(bf16[256,512]{1,0:T(8,128)(2,1)S(1)} %order.1.q_ref), channel_id=1, source_target_pairs={{384,0},{385,1},{386,2},{387,3},{388,4},{389,5},{390,6},{391,7},{3... | collective-permute-start | bytes 786440 | tf_op jit(solution)/shard_map/ppermute | solution.py:326
  19.7 9.4 %collective-permute-start.2 = (bf16[256,256]{1,0:T(8,128)(2,1)S(1)}, bf16[256,256]{1,0:T(8,128)(2,1)S(1)}, u32[]{:S(2)}, u32[]{:S(2)}) collective-permute-start(bf16[256,256]{1,0:T(8,128)(2,1)S(1)} %collective-permute-done.1.a_ref), channel_id=1, source_target_pairs={{0,8},{8,16},{16,24},{24,32},{32,40},{40,48},{48,56},{56,64},{64,7... | collective-permute-start | bytes 393224 | tf_op jit(solution)/shard_map/ppermute | solution.py:320
  21.7 10.6 %collective-permute-start.10 = (bf16[256,256]{1,0:T(8,128)(2,1)S(1)}, bf16[256,256]{1,0:T(8,128)(2,1)S(1)}, u32[]{:S(2)}, u32[]{:S(2)}) collective-permute-start(bf16[256,256]{1,0:T(8,128)(2,1)S(1)} %collective-permute-done.9.b_ref), channel_id=1, source_target_pairs={{0,120},{8,0},{16,8},{24,16},{32,24},{40,32},{48,40},{56,48},{64,5... | collective-permute-start | bytes 393224 | tf_op jit(solution)/shard_map/ppermute | solution.py:322
  25.6 0.7 copy-start.4
  29.2 10.7 %collective-permute-start.3 = (bf16[256,256]{1,0:T(8,128)(2,1)S(1)}, bf16[256,256]{1,0:T(8,128)(2,1)S(1)}, u32[]{:S(2)}, u32[]{:S(2)}) collective-permute-start(bf16[256,256]{1,0:T(8,128)(2,1)S(1)} %collective-permute-done.2.a_ref), channel_id=1, source_target_pairs={{0,8},{8,16},{16,24},{24,32},{32,40},{40,48},{48,56},{56,64},{64,7... | collective-permute-start | bytes 393224 | tf_op jit(solution)/shard_map/ppermute | solution.py:320
  32.3 11.9 %collective-permute-start.11 = (bf16[256,256]{1,0:T(8,128)(2,1)S(1)}, bf16[256,256]{1,0:T(8,128)(2,1)S(1)}, u32[]{:S(2)}, u32[]{:S(2)}) collective-permute-start(bf16[256,256]{1,0:T(8,128)(2,1)S(1)} %collective-permute-done.10.b_ref), channel_id=1, source_target_pairs={{0,120},{8,0},{16,8},{24,16},{32,24},{40,32},{48,40},{56,48},{64,5... | collective-permute-start | bytes 393224 | tf_op jit(solution)/shard_map/ppermute | solution.py:322
  39.9 8.5 %collective-permute-start.4 = (bf16[256,256]{1,0:T(8,128)(2,1)S(1)}, bf16[256,256]{1,0:T(8,128)(2,1)S(1)}, u32[]{:S(2)}, u32[]{:S(2)}) collective-permute-start(bf16[256,256]{1,0:T(8,128)(2,1)S(1)} %collective-permute-done.3.a_ref), channel_id=1, source_target_pairs={{0,8},{8,16},{16,24},{24,32},{32,40},{40,48},{48,56},{56,64},{64,7... | collective-permute-start | bytes 393224 | tf_op jit(solution)/shard_map/ppermute | solution.py:320
  44.3 9.3 %collective-permute-start.12 = (bf16[256,256]{1,0:T(8,128)(2,1)S(1)}, bf16[256,256]{1,0:T(8,128)(2,1)S(1)}, u32[]{:S(2)}, u32[]{:S(2)}) collective-permute-start(bf16[256,256]{1,0:T(8,128)(2,1)S(1)} %collective-permute-done.11.b_ref), channel_id=1, source_target_pairs={{0,120},{8,0},{16,8},{24,16},{32,24},{40,32},{48,40},{56,48},{64,5... | collective-permute-start | bytes 393224 | tf_op jit(solution)/shard_map/ppermute | solution.py:322
  48.4 9.4 %collective-permute-start.5 = (bf16[256,256]{1,0:T(8,128)(2,1)S(1)}, bf16[256,256]{1,0:T(8,128)(2,1)S(1)}, u32[]{:S(2)}, u32[]{:S(2)}) collective-permute-start(bf16[256,256]{1,0:T(8,128)(2,1)S(1)} %collective-permute-done.4.a_ref), channel_id=1, source_target_pairs={{0,8},{8,16},{16,24},{24,32},{32,40},{40,48},{48,56},{56,64},{64,7... | collective-permute-start | bytes 393224 | tf_op jit(solution)/shard_map/ppermute | solution.py:320
  53.5 9.4 %collective-permute-start.13 = (bf16[256,256]{1,0:T(8,128)(2,1)S(1)}, bf16[256,256]{1,0:T(8,128)(2,1)S(1)}, u32[]{:S(2)}, u32[]{:S(2)}) collective-permute-start(bf16[256,256]{1,0:T(8,128)(2,1)S(1)} %collective-permute-done.12.b_ref), channel_id=1, source_target_pairs={{0,120},{8,0},{16,8},{24,16},{32,24},{40,32},{48,40},{56,48},{64,5... | collective-permute-start | bytes 393224 | tf_op jit(solution)/shard_map/ppermute | solution.py:322
  57.8 8.6 %collective-permute-start.6 = (bf16[256,256]{1,0:T(8,128)(2,1)S(1)}, bf16[256,256]{1,0:T(8,128)(2,1)S(1)}, u32[]{:S(2)}, u32[]{:S(2)}) collective-permute-start(bf16[256,256]{1,0:T(8,128)(2,1)S(1)} %collective-permute-done.5.a_ref), channel_id=1, source_target_pairs={{0,8},{8,16},{16,24},{24,32},{32,40},{40,48},{48,56},{56,64},{64,7... | collective-permute-start | bytes 393224 | tf_op jit(solution)/shard_map/ppermute | solution.py:320
  63.0 8.6 %collective-permute-start.14 = (bf16[256,256]{1,0:T(8,128)(2,1)S(1)}, bf16[256,256]{1,0:T(8,128)(2,1)S(1)}, u32[]{:S(2)}, u32[]{:S(2)}) collective-permute-start(bf16[256,256]{1,0:T(8,128)(2,1)S(1)} %collective-permute-done.13.b_ref), channel_id=1, source_target_pairs={{0,120},{8,0},{16,8},{24,16},{32,24},{40,32},{48,40},{56,48},{64,5... | collective-permute-start | bytes 393224 | tf_op jit(solution)/shard_map/ppermute | solution.py:322
  66.4 8.6 %collective-permute-start.7 = (bf16[256,256]{1,0:T(8,128)(2,1)S(1)}, bf16[256,256]{1,0:T(8,128)(2,1)S(1)}, u32[]{:S(2)}, u32[]{:S(2)}) collective-permute-start(bf16[256,256]{1,0:T(8,128)(2,1)S(1)} %collective-permute-done.6.a_ref), channel_id=1, source_target_pairs={{0,8},{8,16},{16,24},{24,32},{32,40},{40,48},{48,56},{56,64},{64,7... | collective-permute-start | bytes 393224 | tf_op jit(solution)/shard_map/ppermute | solution.py:320
  71.6 8.6 %collective-permute-start.15 = (bf16[256,256]{1,0:T(8,128)(2,1)S(1)}, bf16[256,256]{1,0:T(8,128)(2,1)S(1)}, u32[]{:S(2)}, u32[]{:S(2)}) collective-permute-start(bf16[256,256]{1,0:T(8,128)(2,1)S(1)} %collective-permute-done.14.b_ref), channel_id=1, source_target_pairs={{0,120},{8,0},{16,8},{24,16},{32,24},{40,32},{48,40},{56,48},{64,5... | collective-permute-start | bytes 393224 | tf_op jit(solution)/shard_map/ppermute | solution.py:322
  75.0 9.6 %collective-permute-start.8 = (bf16[256,256]{1,0:T(8,128)(2,1)S(1)}, bf16[256,256]{1,0:T(8,128)(2,1)S(1)}, u32[]{:S(2)}, u32[]{:S(2)}) collective-permute-start(bf16[256,256]{1,0:T(8,128)(2,1)S(1)} %collective-permute-done.7.a_ref), channel_id=1, source_target_pairs={{0,8},{8,16},{16,24},{24,32},{32,40},{40,48},{48,56},{56,64},{64,7... | collective-permute-start | bytes 393224 | tf_op jit(solution)/shard_map/ppermute | solution.py:320
  86.1 39.7 %copy-start = (bf16[512,4096]{1,0:T(8,128)(2,1)S(1)}, bf16[512,4096]{1,0:T(8,128)(2,1)}, u32[]{:S(2)}) copy-start(bf16[512,4096]{1,0:T(8,128)(2,1)} %own_w_ref.1) | copy-start | bytes 12582916
  (2 other events, 1.3 us)

commit v2 on v0

--- a/solution.py
+++ b/solution.py
@@ -122,45 +122,59 @@
     fold_masked(info, q_ref, 0, k_ref, v_ref, own_start, acc, top, total)
 
 
+def stack_kernel(q0_ref, q1_ref, q2_ref, q3_ref, out_ref):
+    for slot, ref in enumerate((q0_ref, q1_ref, q2_ref, q3_ref)):
+        out_ref[slot] = ref[...]
+
+
 def step_kernel(
-    distance, last, kinds, sinks, windows, q0_ref, q1_ref, q2_ref, q3_ref, a_ref, b_ref,
-    acc_in, top_in, total_in, acc, top, total, q_ref, k_ref, v_ref
+    distances, last, kinds, sinks, windows, q_ref, a_ref, b_ref,
+    acc_in, top_in, total_in, acc, top, total, k_ref, v_ref
 ):
     del acc_in, top_in, total_in
     info = read_info((kinds, sinks, windows))
     y, z, kind = info[0], info[1], info[2]
     slots = NY - y
-    a_place = lax.rem(z - distance + NZ, NZ)
-    b_place = lax.rem(z + (0 if last else distance), NZ)
-    q_ref[0] = q0_ref[...]
-    q_ref[1] = q1_ref[...]
-    q_ref[2] = q2_ref[...]
-    q_ref[3] = q3_ref[...]
-    split_block(a_ref, k_ref.at[0], v_ref.at[0])
-    split_block(b_ref, k_ref.at[1], v_ref.at[1])
-    a_before = a_place < z
-    b_before = b_place < z
+    places = []
+    for i, distance in enumerate(distances):
+        rows = pl.ds(i * ROWS, ROWS)
+        split_block(a_ref.at[rows], k_ref.at[2 * i], v_ref.at[2 * i])
+        split_block(b_ref.at[rows], k_ref.at[2 * i + 1], v_ref.at[2 * i + 1])
+        places.append(lax.rem(z - distance + NZ, NZ))
+        places.append(lax.rem(z + (0 if last else distance), NZ))
+    before = [place < z for place in places]
 
     @pl.when(kind == 1)
     def _():
-        @pl.loop(jnp.where(a_before | b_before, 0, 1), slots)
+        any_before = functools.reduce(jnp.logical_or, before)
+
+        @pl.loop(jnp.where(any_before, 0, 1), slots)
         def _(slot):
-            valid = [(slot > 0) | a_before, (slot > 0) | b_before]
-            fold(q_ref, slot, [k_ref[0], k_ref[1]], [v_ref[0], v_ref[1]], None, valid, acc, top, total)
+            for i in range(0, len(places), 2):
+                sides = (i, i + 1)
+                valid = [(slot > 0) | before[n] for n in sides]
+                keys, values = [k_ref[n] for n in sides], [v_ref[n] for n in sides]
+                fold(q_ref, slot, keys, values, None, valid, acc, top, total)
 
     @pl.when(kind != 1)
     def _():
-        @pl.loop(0, 2 * slots)
+        blocks = len(places)
+
+        @pl.loop(0, blocks * slots)
         def _(n):
-            slot = n // 2
-            side = n % 2
-            place = jnp.where(side == 0, a_place, b_place)
+            slot = n // blocks
+            side = n % blocks
+            place = places[0]
+            for i in range(1, blocks):
+                place = jnp.where(side == i, places[i], place)
             skip = (slot == 0) & (place == z)
 
             @pl.when(jnp.logical_not(skip))
             def _():
                 key_start = y * ROW_KEYS + place * ROWS
-                fold_masked(info, q_ref, slot, k_ref.at[side], v_ref.at[side], key_start, acc, top, total)
+                fold_masked(
+                    info, q_ref, slot, k_ref.at[side], v_ref.at[side], key_start, acc, top, total
+                )
 
 
 def finish_kernel(acc, top, total, out_ref):
@@ -234,12 +248,16 @@
     return pltpu.CompilerParams(vmem_limit_bytes=mib << 20)
 
 
+ROUNDS = {1: (1, (1,)), 2: (2, (2, 3)), 3: (2, (4, 5)), 4: (2, (6, 7)), 5: (1, (8,))}
+
+
 def body(queries, keys, values, head_kind, sink_len, window_len, w_out):
     heads = (head_kind, sink_len, window_len)
     own = pl.pallas_call(
         pack_kernel,
+        grid=(1,),
         out_shape=jax.ShapeDtypeStruct((ROWS, 2 * HD), jnp.bfloat16),
-        in_specs=[VMEM_SPEC] * 2,
+        in_specs=[pl.BlockSpec((ROWS, HD), lambda i: (0, 0))] * 2,
         out_specs=VMEM_SPEC,
         compiler_params=params(),
         name="pack",
@@ -253,9 +271,6 @@
         name="order",
     )(queries)
 
-    ahead = [(i, (i + 1) % NZ) for i in range(NZ)]
-    behind = [(i, (i - 1) % NZ) for i in range(NZ)]
-    half = NZ // 2
     a, b = {0: own}, {0: own}
     cost = pl.CostEstimate(flops=1 << 30, bytes_accessed=8 << 20, transcendentals=1 << 22)
     state = pl.pallas_call(
@@ -269,32 +284,46 @@
         name="first",
     )(*heads, queries[None], own)
 
-    for d in range(1, half + 1):
-        a[d] = lax.ppermute(a[d - 1], "z", ahead)
-        if d < half:
-            b[d] = lax.ppermute(b[d - 1], "z", behind)
-    b[half] = own
+    final = len(ROUNDS)
+    send_a = send_b = own
+    for d, (hops, _) in ROUNDS.items():
+        a[d] = lax.ppermute(send_a, "z", [(i, (i + hops) % NZ) for i in range(NZ)])
+        send_a = jnp.concatenate([own, a[1]], axis=0) if d == 1 else a[d]
+        if d == final:
+            b[d] = own
+            break
+        b[d] = lax.ppermute(send_b, "z", [(i, (i - hops) % NZ) for i in range(NZ)])
+        send_b = jnp.concatenate([own, b[1]], axis=0) if d == 1 else b[d]
+        if d + 1 == final:
+            send_a = a[d][ROWS:]
     received = []
     for k in range(1, NY):
         received.append(lax.ppermute(queries, "y", [(i, i - k) for i in range(k, NY)]))
     other_w = lax.ppermute(w_out, "core", [(0, 1), (1, 0)])
 
-    for d in range(1, half + 1):
+    slots = pl.pallas_call(
+        stack_kernel,
+        out_shape=jax.ShapeDtypeStruct((NY, ROWS, GROUP * HD), jnp.bfloat16),
+        in_specs=[VMEM_SPEC] * NY,
+        out_specs=VMEM_SPEC,
+        compiler_params=params(),
+        name="stack",
+    )(queries, *received)
+    for d, (_, distances) in ROUNDS.items():
         state = pl.pallas_call(
-            functools.partial(step_kernel, d, d == half),
+            functools.partial(step_kernel, distances, d == final),
             out_shape=STATE,
-            in_specs=[SMEM_SPEC] * 3 + [VMEM_SPEC] * 9,
+            in_specs=[SMEM_SPEC] * 3 + [VMEM_SPEC] * 6,
             out_specs=[VMEM_SPEC] * 3,
             scratch_shapes=[
-                pltpu.VMEM((NY, ROWS, GROUP * HD), jnp.bfloat16),
-                pltpu.VMEM((2, ROWS, HD), jnp.bfloat16),
-                pltpu.VMEM((2, HD, ROWS), jnp.bfloat16),
+                pltpu.VMEM((2 * len(distances), ROWS, HD), jnp.bfloat16),
+                pltpu.VMEM((2 * len(distances), HD, ROWS), jnp.bfloat16),
             ],
-            input_output_aliases={9: 0, 10: 1, 11: 2},
+            input_output_aliases={6: 0, 7: 1, 8: 2},
             compiler_params=params(),
             cost_estimate=cost,
             name="step",
-        )(*heads, queries, *received, a[d], b[d], *state)
+        )(*heads, slots, a[d], b[d], *state)
 
     packed = pl.pallas_call(
         finish_kernel,

time: 152 us -> 143 us (0.941)
  the two profiles are of different devices: /device:TPU:224 before, /device:TPU:256 now
where the time goes in v2:
time: 143 us
  blocking collectives  63.7 us (45%)
  starting transfers between devices  42.1 us (29%)
  Pallas kernels  16.8 us (12%)
  waiting for transfers between devices  14.4 us (10%)
  local copies, waits for them, and re-layouts  4.59 us (3%)
    all_to_all x1, blocking collectives, body(): parts = lax.all_to_all(packed, ('y', 'core'), 0, 0, tiled=True)  38.3 us
    all_to_all x1, blocking collectives, body(): pieces = lax.all_to_all(mixed.reshape(NX, 32, -1), 'x', 0, 0, tiled=True)  25.4 us
    ppermute x4, starting transfers between devices, body(): b[d] = lax.ppermute(send_b, 'z', [(i, (i - hops) % NZ) for i in range(NZ)])  19.1 us
    ppermute x5, starting transfers between devices, body(): a[d] = lax.ppermute(send_a, 'z', [(i, (i + hops) % NZ) for i in range(NZ)])  17.2 us
    ppermute x5, waiting for transfers between devices, body(): a[d] = lax.ppermute(send_a, 'z', [(i, (i + hops) % NZ) for i in range(NZ)])  13 us
    pallas_call x5, Pallas kernels, body(): pl.pallas_call(functools.partial(step_kernel, distances, d == final), out...  11.9 us
    unnamed x14, local copies, waits for them, and re-layouts  4.58 us
    ppermute x3, starting transfers between devices, body(): lax.ppermute(queries, 'y', [(i, i - k) for i in range(k, NY)])  3.88 us
  transfers between devices with their start and end apart: 13, of which 4 were waited for; matrix products, arithmetic and copies ran while one was open for 0% of the time, Pallas kernels for 10%

profile of v2, /device:TPU:256, one launch (start us, length us, event | category | flops | bytes accessed | tf_op | source)
XLA Modules:
  0.0 142.9 jit_solution(8441002860071079424)
XLA Ops:
  0.0 1.9 %collective-permute-start.12 = (bf16[512,4096]{1,0:T(8,128)(2,1)}, bf16[512,4096]{1,0:T(8,128)(2,1)S(1)}, u32[]{:S(2)}, u32[]{:S(2)}) collective-permute-start(bf16[512,4096]{1,0:T(8,128)(2,1)} %own_w_ref.1), channel_id=1, source_target_pairs={{0,1},{1,0},{2,3},{3,2},{4,5},{5,4},{6,7},{7,6},{8,9},{9,8},{10,11... | collective-permute-start | bytes 12582920 | tf_op jit(solution)/shard_map/ppermute | solution.py:302
  3.7 2.9 %collective-permute-start.3 = (bf16[256,256]{1,0:T(8,128)(2,1)S(1)}, bf16[256,256]{1,0:T(8,128)(2,1)S(1)}, u32[]{:S(2)}, u32[]{:S(2)}) collective-permute-start(bf16[256,256]{1,0:T(8,128)(2,1)S(1)} %pack.1.own_ref.b_ref), channel_id=1, source_target_pairs={{0,8},{8,16},{16,24},{24,32},{32,40},{40,48},{48,56},{56,64},{64,7... | collective-permute-start | bytes 393224 | tf_op jit(solution)/shard_map/ppermute | solution.py:290
  6.6 4.1 %collective-permute-start.8 = (bf16[256,256]{1,0:T(8,128)(2,1)S(1)}, bf16[256,256]{1,0:T(8,128)(2,1)S(1)}, u32[]{:S(2)}, u32[]{:S(2)}) collective-permute-start(bf16[256,256]{1,0:T(8,128)(2,1)S(1)} %pack.1.own_ref.b_ref), channel_id=1, source_target_pairs={{0,120},{8,0},{16,8},{24,16},{32,24},{40,32},{48,40},{56,48},{64,5... | collective-permute-start | bytes 393224 | tf_op jit(solution)/shard_map/ppermute | solution.py:295
  10.8 1.9 %collective-permute-done.3.a_ref = bf16[256,256]{1,0:T(8,128)(2,1)S(1)} collective-permute-done((bf16[256,256]{1,0:T(8,128)(2,1)S(1)}, bf16[256,256]{1,0:T(8,128)(2,1)S(1)}, u32[]{:S(2)}, u32[]{:S(2)}) %collective-permute-start.3) | collective-permute-done | bytes 131104 | tf_op jit(solution)/shard_map/ppermute | solution.py:290
  12.7 1.4 %collective-permute-done.8.b_ref = bf16[256,256]{1,0:T(8,128)(2,1)S(1)} collective-permute-done((bf16[256,256]{1,0:T(8,128)(2,1)S(1)}, bf16[256,256]{1,0:T(8,128)(2,1)S(1)}, u32[]{:S(2)}, u32[]{:S(2)}) %collective-permute-start.8) | collective-permute-done | bytes 131104 | tf_op jit(solution)/shard_map/ppermute | solution.py:295
  14.2 3.4 %collective-permute-start.4 = (bf16[512,256]{1,0:T(8,128)(2,1)S(1)}, bf16[512,256]{1,0:T(8,128)(2,1)S(1)}, u32[]{:S(2)}, u32[]{:S(2)}) collective-permute-start(bf16[512,256]{1,0:T(8,128)(2,1)S(1)} %get-tuple-element.42), channel_id=1, source_target_pairs={{0,16},{8,24},{16,32},{24,40},{32,48},{40,56},{48,64},{56,72},{64,... | collective-permute-start | bytes 786440 | tf_op jit(solution)/shard_map/ppermute | solution.py:290
  18.6 1.3 collective-permute-start
  19.9 4.6 %collective-permute-start.9 = (bf16[512,256]{1,0:T(8,128)(2,1)S(1)}, bf16[512,256]{1,0:T(8,128)(2,1)S(1)}, u32[]{:S(2)}, u32[]{:S(2)}) collective-permute-start(bf16[512,256]{1,0:T(8,128)(2,1)S(1)} %get-tuple-element.41), channel_id=1, source_target_pairs={{0,112},{8,120},{16,0},{24,8},{32,16},{40,24},{48,32},{56,40},{64,... | collective-permute-start | bytes 786440 | tf_op jit(solution)/shard_map/ppermute | solution.py:295
  24.5 7.3 %collective-permute-done.4.a_ref = bf16[512,256]{1,0:T(8,128)(2,1)S(1)} collective-permute-done((bf16[512,256]{1,0:T(8,128)(2,1)S(1)}, bf16[512,256]{1,0:T(8,128)(2,1)S(1)}, u32[]{:S(2)}, u32[]{:S(2)}) %collective-permute-start.4) | collective-permute-done | bytes 262176 | tf_op jit(solution)/shard_map/ppermute | solution.py:290
  31.7 1.9 %collective-permute-start.5 = (bf16[512,256]{1,0:T(8,128)(2,1)S(1)}, bf16[512,256]{1,0:T(8,128)(2,1)S(1)}, u32[]{:S(2)}, u32[]{:S(2)}) collective-permute-start(bf16[512,256]{1,0:T(8,128)(2,1)S(1)} %collective-permute-done.4.a_ref), channel_id=1, source_target_pairs={{0,16},{8,24},{16,32},{24,40},{32,48},{40,56},{48,64},{56,72},{64,... | collective-permute-start | bytes 786440 | tf_op jit(solution)/shard_map/ppermute | solution.py:290
  33.6 1.3 collective-permute-start.1
  36.3 6.0 %collective-permute-start.10 = (bf16[512,256]{1,0:T(8,128)(2,1)S(1)}, bf16[512,256]{1,0:T(8,128)(2,1)S(1)}, u32[]{:S(2)}, u32[]{:S(2)}) collective-permute-start(bf16[512,256]{1,0:T(8,128)(2,1)S(1)} %collective-permute-done.9.b_ref), channel_id=1, source_target_pairs={{0,112},{8,120},{16,0},{24,8},{32,16},{40,24},{48,32},{56,40},{64,... | collective-permute-start | bytes 786440 | tf_op jit(solution)/shard_map/ppermute | solution.py:295
  42.3 3.8 %collective-permute-done.5.a_ref = bf16[512,256]{1,0:T(8,128)(2,1)S(1)} collective-permute-done((bf16[512,256]{1,0:T(8,128)(2,1)S(1)}, bf16[512,256]{1,0:T(8,128)(2,1)S(1)}, u32[]{:S(2)}, u32[]{:S(2)}) %collective-permute-start.5) | collective-permute-done | bytes 262176 | tf_op jit(solution)/shard_map/ppermute | solution.py:290
  46.1 3.6 %collective-permute-start.6 = (bf16[512,256]{1,0:T(8,128)(2,1)S(1)}, bf16[512,256]{1,0:T(8,128)(2,1)S(1)}, u32[]{:S(2)}, u32[]{:S(2)}) collective-permute-start(bf16[512,256]{1,0:T(8,128)(2,1)S(1)} %collective-permute-done.5.a_ref), channel_id=1, source_target_pairs={{0,16},{8,24},{16,32},{24,40},{32,48},{40,56},{48,64},{56,72},{64,... | collective-permute-start | bytes 786440 | tf_op jit(solution)/shard_map/ppermute | solution.py:290
  51.6 1.6 %first.1 = (f32[4,4,128,256]{3,2,1,0:T(8,128)S(1)}, f32[4,4,8,256]{3,2,1,0:T(8,128)S(1)}, f32[4,4,8,256]{3,2,1,0:T(8,128)S(1)}) custom-call(s32[8]{0:T(128)S(1)} %copy-done.4, s32[8]{0:T(128)S(1)} %copy-done.5, s32[8]{0:T(128)S(1)} %copy-done.6, bf16[1,256,512]{2,1,0:T(8,128)(2,1)S(1)} %bitcast.3, bf16[256,256]{1,0:T(8,128)(2,1)S(1)} %pack.1.own_ref.b_ref), custom_call_target="tpu_custom_call" | custom-call | flops 1073741824 | bytes 8388608 | tf_op jit(solution)/shard_map/first/pallas_call | solution.py:276
  53.4 4.3 %collective-permute-start.11 = (bf16[512,256]{1,0:T(8,128)(2,1)S(1)}, bf16[512,256]{1,0:T(8,128)(2,1)S(1)}, u32[]{:S(2)}, u32[]{:S(2)}) collective-permute-start(bf16[512,256]{1,0:T(8,128)(2,1)S(1)} %collective-permute-done.10.b_ref), channel_id=1, source_target_pairs={{0,112},{8,120},{16,0},{24,8},{32,16},{40,24},{48,32},{56,40},{64,... | collective-permute-start | bytes 786440 | tf_op jit(solution)/shard_map/ppermute | solution.py:295
  57.7 1.7 %step.5 = (f32[4,4,128,256]{3,2,1,0:T(8,128)S(1)}, f32[4,4,8,256]{3,2,1,0:T(8,128)S(1)}, f32[4,4,8,256]{3,2,1,0:T(8,128)S(1)}) custom-call(s32[8]{0:T(128)S(1)} %copy-done.4, s32[8]{0:T(128)S(1)} %copy-done.5, s32[8]{0:T(128)S(1)} %copy-done.6, bf16[4,256,512]{2,1,0:T(8,128)(2,1)S(1)} %stack.1.q_ref, ...), custom_call_target="tpu_custom_call", output_to_operand_aliasing={{0}: (6, {}), {1}: (7, {}), {2}: (8, {})} | custom-call | flops 1073741824 | bytes 8388608 | tf_op jit(solution)/shard_map/step/pallas_call | solution.py:313
  59.4 2.8 %step.6 = (f32[4,4,128,256]{3,2,1,0:T(8,128)S(1)}, f32[4,4,8,256]{3,2,1,0:T(8,128)S(1)}, f32[4,4,8,256]{3,2,1,0:T(8,128)S(1)}) custom-call(s32[8]{0:T(128)S(1)} %copy-done.4, s32[8]{0:T(128)S(1)} %copy-done.5, s32[8]{0:T(128)S(1)} %copy-done.6, bf16[4,256,512]{2,1,0:T(8,128)(2,1)S(1)} %stack.1.q_ref, ...), custom_call_target="tpu_custom_call", output_to_operand_aliasing={{0}: (6, {}), {1}: (7, {}), {2}: (8, {})} | custom-call | flops 1073741824 | bytes 8388608 | tf_op jit(solution)/shard_map/step/pallas_call | solution.py:313
  62.2 5.4 %collective-permute-start.7 = (bf16[256,256]{1,0:T(8,128)(2,1)S(1)}, bf16[256,256]{1,0:T(8,128)(2,1)S(1)}, u32[]{:S(2)}, u32[]{:S(2)}) collective-permute-start(bf16[256,256]{1,0:T(8,128)(2,1)S(1)} %slice.4), channel_id=1, source_target_pairs={{0,8},{8,16},{16,24},{24,32},{32,40},{40,48},{48,56},{56,64},{64,7... | collective-permute-start | bytes 393224 | tf_op jit(solution)/shard_map/ppermute | solution.py:290
  67.6 1.9 %step.7 = (f32[4,4,128,256]{3,2,1,0:T(8,128)S(1)}, f32[4,4,8,256]{3,2,1,0:T(8,128)S(1)}, f32[4,4,8,256]{3,2,1,0:T(8,128)S(1)}) custom-call(s32[8]{0:T(128)S(1)} %copy-done.4, s32[8]{0:T(128)S(1)} %copy-done.5, s32[8]{0:T(128)S(1)} %copy-done.6, bf16[4,256,512]{2,1,0:T(8,128)(2,1)S(1)} %stack.1.q_ref, ...), custom_call_target="tpu_custom_call", output_to_operand_aliasing={{0}: (6, {}), {1}: (7, {}), {2}: (8, {})} | custom-call | flops 1073741824 | bytes 8388608 | tf_op jit(solution)/shard_map/step/pallas_call | solution.py:313
  70.8 4.3 %step.9 = (f32[4,4,128,256]{3,2,1,0:T(8,128)S(1)}, f32[4,4,8,256]{3,2,1,0:T(8,128)S(1)}, f32[4,4,8,256]{3,2,1,0:T(8,128)S(1)}) custom-call(s32[8]{0:T(128)S(1)} %copy-done.4, s32[8]{0:T(128)S(1)} %copy-done.5, s32[8]{0:T(128)S(1)} %copy-done.6, bf16[4,256,512]{2,1,0:T(8,128)(2,1)S(1)} %stack.1.q_ref, ...), custom_call_target="tpu_custom_call", output_to_operand_aliasing={{0}: (6, {}), {1}: (7, {}), {2}: (8, {})} | custom-call | flops 1073741824 | bytes 8388608 | tf_op jit(solution)/shard_map/step/pallas_call | solution.py:313
  75.4 38.3 %all_to_all.10.parts_ref = bf16[8,528,128]{2,1,0:T(8,128)(2,1)S(1)} all-to-all(bf16[8,528,128]{2,1,0:T(8,128)(2,1)S(1)} %finish.1), channel_id=1, replica_groups=mesh['y'=4,'z'=16,'x'=4,'core'=2] {'y','core'}, dimensions={0} | all-to-all | bytes 2162688 | tf_op jit(solution)/shard_map/all_to_all | solution.py:336
  113.7 2.8 %project.1 = bf16[128,4096]{1,0:T(8,128)(2,1)S(1)} custom-call(bf16[8,528,128]{2,1,0:T(8,128)(2,1)S(1)} %all_to_all.10.parts_ref, bf16[512,4096]{1,0:T(8,128)(2,1)S(1)} %copy-done, bf16[512,4096]{1,0:T(8,128)(2,1)S(1)} %collective-permute-done.12.other_w_ref), custom_call_target="tpu_custom_call" | custom-call | tf_op jit(solution)/shard_map/project/pallas_call | solution.py:339
  116.5 25.4 %all_to_all.11 = bf16[4,32,4096]{2,1,0:T(8,128)(2,1)S(1)} all-to-all(bf16[4,32,4096]{2,1,0:T(8,128)(2,1)S(1)} %bitcast.2), channel_id=1, replica_groups=mesh['y'=4,'z'=16,'x'=4,'core'=2] {'x'}, dimensions={0} | all-to-all | bytes 2097152 | tf_op jit(solution)/shard_map/all_to_all | solution.py:353
  (32 shorter events, 8.6 us)
Async XLA Ops:
  0.0 113.7 %collective-permute-start.12 = (bf16[512,4096]{1,0:T(8,128)(2,1)}, bf16[512,4096]{1,0:T(8,128)(2,1)S(1)}, u32[]{:S(2)}, u32[]{:S(2)}) collective-permute-start(bf16[512,4096]{1,0:T(8,128)(2,1)} %own_w_ref.1), channel_id=1, source_target_pairs={{0,1},{1,0},{2,3},{3,2},{4,5},{5,4},{6,7},{7,6},{8,9},{9,8},{10,11... | collective-permute-start | bytes 12582920 | tf_op jit(solution)/shard_map/ppermute | solution.py:302
  1.9 0.8 copy-start.2
  2.8 0.8 copy-start.3
  3.7 9.0 %collective-permute-start.3 = (bf16[256,256]{1,0:T(8,128)(2,1)S(1)}, bf16[256,256]{1,0:T(8,128)(2,1)S(1)}, u32[]{:S(2)}, u32[]{:S(2)}) collective-permute-start(bf16[256,256]{1,0:T(8,128)(2,1)S(1)} %pack.1.own_ref.b_ref), channel_id=1, source_target_pairs={{0,8},{8,16},{16,24},{24,32},{32,40},{40,48},{48,56},{56,64},{64,7... | collective-permute-start | bytes 393224 | tf_op jit(solution)/shard_map/ppermute | solution.py:290
  6.6 7.5 %collective-permute-start.8 = (bf16[256,256]{1,0:T(8,128)(2,1)S(1)}, bf16[256,256]{1,0:T(8,128)(2,1)S(1)}, u32[]{:S(2)}, u32[]{:S(2)}) collective-permute-start(bf16[256,256]{1,0:T(8,128)(2,1)S(1)} %pack.1.own_ref.b_ref), channel_id=1, source_target_pairs={{0,120},{8,0},{16,8},{24,16},{32,24},{40,32},{48,40},{56,48},{64,5... | collective-permute-start | bytes 393224 | tf_op jit(solution)/shard_map/ppermute | solution.py:295
  14.2 17.5 %collective-permute-start.4 = (bf16[512,256]{1,0:T(8,128)(2,1)S(1)}, bf16[512,256]{1,0:T(8,128)(2,1)S(1)}, u32[]{:S(2)}, u32[]{:S(2)}) collective-permute-start(bf16[512,256]{1,0:T(8,128)(2,1)S(1)} %get-tuple-element.42), channel_id=1, source_target_pairs={{0,16},{8,24},{16,32},{24,40},{32,48},{40,56},{48,64},{56,72},{64,... | collective-permute-start | bytes 786440 | tf_op jit(solution)/shard_map/ppermute | solution.py:290
  17.6 1.0 copy-start.1
  18.6 16.4 %collective-permute-start = (bf16[256,512]{1,0:T(8,128)(2,1)S(1)}, bf16[256,512]{1,0:T(8,128)(2,1)S(1)}, u32[]{:S(2)}, u32[]{:S(2)}) collective-permute-start(bf16[256,512]{1,0:T(8,128)(2,1)S(1)} %order.1.q0_ref), channel_id=1, source_target_pairs={{128,0},{256,128},{384,256},{129,1},{257,129},{385,257},{130,2},{2... | collective-permute-start | bytes 786440 | tf_op jit(solution)/shard_map/ppermute | solution.py:301
  19.9 16.4 %collective-permute-start.9 = (bf16[512,256]{1,0:T(8,128)(2,1)S(1)}, bf16[512,256]{1,0:T(8,128)(2,1)S(1)}, u32[]{:S(2)}, u32[]{:S(2)}) collective-permute-start(bf16[512,256]{1,0:T(8,128)(2,1)S(1)} %get-tuple-element.41), channel_id=1, source_target_pairs={{0,112},{8,120},{16,0},{24,8},{32,16},{40,24},{48,32},{56,40},{64,... | collective-permute-start | bytes 786440 | tf_op jit(solution)/shard_map/ppermute | solution.py:295
  31.7 14.4 %collective-permute-start.5 = (bf16[512,256]{1,0:T(8,128)(2,1)S(1)}, bf16[512,256]{1,0:T(8,128)(2,1)S(1)}, u32[]{:S(2)}, u32[]{:S(2)}) collective-permute-start(bf16[512,256]{1,0:T(8,128)(2,1)S(1)} %collective-permute-done.4.a_ref), channel_id=1, source_target_pairs={{0,16},{8,24},{16,32},{24,40},{32,48},{40,56},{48,64},{56,72},{64,... | collective-permute-start | bytes 786440 | tf_op jit(solution)/shard_map/ppermute | solution.py:290
  33.6 19.6 %collective-permute-start.1 = (bf16[256,512]{1,0:T(8,128)(2,1)S(1)}, bf16[256,512]{1,0:T(8,128)(2,1)S(1)}, u32[]{:S(2)}, u32[]{:S(2)}) collective-permute-start(bf16[256,512]{1,0:T(8,128)(2,1)S(1)} %order.1.q0_ref), channel_id=1, source_target_pairs={{256,0},{384,128},{257,1},{385,129},{258,2},{386,130},{259,3},{387... | collective-permute-start | bytes 786440 | tf_op jit(solution)/shard_map/ppermute | solution.py:301
  35.0 18.3 %collective-permute-start.2 = (bf16[256,512]{1,0:T(8,128)(2,1)S(1)}, bf16[256,512]{1,0:T(8,128)(2,1)S(1)}, u32[]{:S(2)}, u32[]{:S(2)}) collective-permute-start(bf16[256,512]{1,0:T(8,128)(2,1)S(1)} %order.1.q0_ref), channel_id=1, source_target_pairs={{384,0},{385,1},{386,2},{387,3},{388,4},{389,5},{390,6},{391,7},{3... | collective-permute-start | bytes 786440 | tf_op jit(solution)/shard_map/ppermute | solution.py:301
  36.3 17.1 %collective-permute-start.10 = (bf16[512,256]{1,0:T(8,128)(2,1)S(1)}, bf16[512,256]{1,0:T(8,128)(2,1)S(1)}, u32[]{:S(2)}, u32[]{:S(2)}) collective-permute-start(bf16[512,256]{1,0:T(8,128)(2,1)S(1)} %collective-permute-done.9.b_ref), channel_id=1, source_target_pairs={{0,112},{8,120},{16,0},{24,8},{32,16},{40,24},{48,32},{56,40},{64,... | collective-permute-start | bytes 786440 | tf_op jit(solution)/shard_map/ppermute | solution.py:295
  46.1 16.1 %collective-permute-start.6 = (bf16[512,256]{1,0:T(8,128)(2,1)S(1)}, bf16[512,256]{1,0:T(8,128)(2,1)S(1)}, u32[]{:S(2)}, u32[]{:S(2)}) collective-permute-start(bf16[512,256]{1,0:T(8,128)(2,1)S(1)} %collective-permute-done.5.a_ref), channel_id=1, source_target_pairs={{0,16},{8,24},{16,32},{24,40},{32,48},{40,56},{48,64},{56,72},{64,... | collective-permute-start | bytes 786440 | tf_op jit(solution)/shard_map/ppermute | solution.py:290
  49.7 0.7 copy-start.4
  50.3 0.7 copy-start.5
  51.0 0.7 copy-start.6
  53.4 16.2 %collective-permute-start.11 = (bf16[512,256]{1,0:T(8,128)(2,1)S(1)}, bf16[512,256]{1,0:T(8,128)(2,1)S(1)}, u32[]{:S(2)}, u32[]{:S(2)}) collective-permute-start(bf16[512,256]{1,0:T(8,128)(2,1)S(1)} %collective-permute-done.10.b_ref), channel_id=1, source_target_pairs={{0,112},{8,120},{16,0},{24,8},{32,16},{40,24},{48,32},{56,40},{64,... | collective-permute-start | bytes 786440 | tf_op jit(solution)/shard_map/ppermute | solution.py:295
  62.2 8.6 %collective-permute-start.7 = (bf16[256,256]{1,0:T(8,128)(2,1)S(1)}, bf16[256,256]{1,0:T(8,128)(2,1)S(1)}, u32[]{:S(2)}, u32[]{:S(2)}) collective-permute-start(bf16[256,256]{1,0:T(8,128)(2,1)S(1)} %slice.4), channel_id=1, source_target_pairs={{0,8},{8,16},{16,24},{24,32},{32,40},{40,48},{48,56},{56,64},{64,7... | collective-permute-start | bytes 393224 | tf_op jit(solution)/shard_map/ppermute | solution.py:290
  75.1 38.6 %copy-start = (bf16[512,4096]{1,0:T(8,128)(2,1)S(1)}, bf16[512,4096]{1,0:T(8,128)(2,1)}, u32[]{:S(2)}) copy-start(bf16[512,4096]{1,0:T(8,128)(2,1)} %own_w_ref.1) | copy-start | bytes 12582916

commit v3 on v2

--- a/solution.py
+++ b/solution.py
@@ -20,6 +20,7 @@
 SCALE = 1.0 / math.sqrt(HD)
 EXP2_SCALE = SCALE * math.log2(math.e)
 STAT_ROWS = 16
+CHUNK = 64
 PACK = GROUP * HD + STAT_ROWS
 NT = (((1,), (1,)), ((), ()))
 
@@ -43,18 +44,15 @@
     return ((col % 128) // 32 * NC + col // 128) * 32 + col % 32
 
 
-def fold(q_ref, slot, keys, values, mask, valid, acc, top, total):
+def fold(q_ref, slot, keys, values, mask, valid, acc, top, total, s_ref):
     def score(h):
         q = q_ref[slot, :, h * HD : (h + 1) * HD]
-        out = []
-        for k in keys:
+        new = top[slot, h]
+        for n, k in enumerate(keys):
             s = lax.dot_general(k, q, NT, preferred_element_type=jnp.float32)
-            out.append(s if mask is None else jnp.where(mask, s, MASKED))
-        return out
-
-    def peaks(h, scores):
-        new = top[slot, h]
-        for n, s in enumerate(scores):
+            if mask is not None:
+                s = jnp.where(mask, s, MASKED)
+            s_ref[h % 2, n] = s
             peak = jnp.max(s.reshape(ROWS // 8, 8, ROWS), axis=0)
             peak = jnp.max(peak, axis=0, keepdims=True)
             if valid is not None:
@@ -62,23 +60,22 @@
             new = jnp.maximum(new, peak)
         return new
 
-    scores = score(0)
-    new = peaks(0, scores)
+    new = score(0)
     for h in range(GROUP):
         if h + 1 < GROUP:
-            scores_next = score(h + 1)
-            new_next = peaks(h + 1, scores_next)
+            new_next = score(h + 1)
         old = top[slot, h]
         factor = jnp.exp2((old - new) * EXP2_SCALE)
         part = total[slot, h] * factor
         weights = []
-        for n, s in enumerate(scores):
+        for n in range(len(keys)):
             shift = new[:1] * EXP2_SCALE
             if valid is not None:
                 shift = jnp.where(valid[n], shift, -MASKED)
-            w = jnp.exp2(s * EXP2_SCALE - shift)
-            part = part + jnp.sum(w.reshape(ROWS // 8, 8, ROWS), axis=0)
-            weights.append(w.astype(jnp.bfloat16))
+            for r in range(0, ROWS, CHUNK):
+                w = jnp.exp2(s_ref[h % 2, n, r : r + CHUNK] * EXP2_SCALE - shift)
+                part = part + jnp.sum(w.reshape(CHUNK // 8, 8, ROWS), axis=0)
+                weights.append(w.astype(jnp.bfloat16))
         out = jnp.dot(
             jnp.concatenate(values, axis=1),
             jnp.concatenate(weights, axis=0),
@@ -88,7 +85,7 @@
         total[slot, h] = part
         acc[slot, h] = acc[slot, h] * factor[:1] + out
         if h + 1 < GROUP:
-            scores, new = scores_next, new_next
+            new = new_next
 
 
 def split_block(block_ref, k_ref, v_ref):
@@ -97,7 +94,7 @@
     v_ref[:, HD:] = block_ref[HD:, HD:]
 
 
-def fold_masked(info, q_ref, slot, k_ref, v_ref, key_start, acc, top, total):
+def fold_masked(info, q_ref, slot, k_ref, v_ref, key_start, acc, top, total, s_ref):
     kind, sink, window = info[2], info[3], info[4]
     query_start = (info[0] + slot) * ROW_KEYS + info[1] * ROWS
     needed = (key_start <= query_start + ROWS - 1) & (
@@ -109,17 +106,17 @@
         i = query_start + query_offsets((ROWS, ROWS))
         j = key_start + lax.broadcasted_iota(jnp.int32, (ROWS, ROWS), 0)
         mask = (j <= i) & ((kind == 1) | (j > i - window) | (j < sink))
-        fold(q_ref, slot, [k_ref[...]], [v_ref[...]], mask, None, acc, top, total)
-
-
-def first_kernel(kinds, sinks, windows, q_ref, own_ref, acc, top, total, k_ref, v_ref):
+        fold(q_ref, slot, [k_ref[...]], [v_ref[...]], mask, None, acc, top, total, s_ref)
+
+
+def first_kernel(kinds, sinks, windows, q_ref, own_ref, acc, top, total, k_ref, v_ref, s_ref):
     info = read_info((kinds, sinks, windows))
     acc[...] = jnp.zeros_like(acc)
     top[...] = jnp.full_like(top, LOW)
     total[...] = jnp.zeros_like(total)
     own_start = info[0] * ROW_KEYS + info[1] * ROWS
     split_block(own_ref, k_ref, v_ref)
-    fold_masked(info, q_ref, 0, k_ref, v_ref, own_start, acc, top, total)
+    fold_masked(info, q_ref, 0, k_ref, v_ref, own_start, acc, top, total, s_ref)
 
 
 def stack_kernel(q0_ref, q1_ref, q2_ref, q3_ref, out_ref):
@@ -129,7 +126,7 @@
 
 def step_kernel(
     distances, last, kinds, sinks, windows, q_ref, a_ref, b_ref,
-    acc_in, top_in, total_in, acc, top, total, k_ref, v_ref
+    acc_in, top_in, total_in, acc, top, total, k_ref, v_ref, s_ref
 ):
     del acc_in, top_in, total_in
     info = read_info((kinds, sinks, windows))
@@ -154,7 +151,7 @@
                 sides = (i, i + 1)
                 valid = [(slot > 0) | before[n] for n in sides]
                 keys, values = [k_ref[n] for n in sides], [v_ref[n] for n in sides]
-                fold(q_ref, slot, keys, values, None, valid, acc, top, total)
+                fold(q_ref, slot, keys, values, None, valid, acc, top, total, s_ref)
 
     @pl.when(kind != 1)
     def _():
@@ -173,7 +170,7 @@
             def _():
                 key_start = y * ROW_KEYS + place * ROWS
                 fold_masked(
-                    info, q_ref, slot, k_ref.at[side], v_ref.at[side], key_start, acc, top, total
+                    info, q_ref, slot, k_ref.at[side], v_ref.at[side], key_start, acc, top, total, s_ref
                 )
 
 
@@ -278,7 +275,11 @@
         out_shape=STATE,
         in_specs=[SMEM_SPEC] * 3 + [VMEM_SPEC] * 2,
         out_specs=[VMEM_SPEC] * 3,
-        scratch_shapes=[pltpu.VMEM((ROWS, HD), jnp.bfloat16), pltpu.VMEM((HD, ROWS), jnp.bfloat16)],
+        scratch_shapes=[
+            pltpu.VMEM((ROWS, HD), jnp.bfloat16),
+            pltpu.VMEM((HD, ROWS), jnp.bfloat16),
+            pltpu.VMEM((2, 2, ROWS, ROWS), jnp.float32),
+        ],
         compiler_params=params(),
         cost_estimate=cost,
         name="first",
@@ -318,6 +319,7 @@
             scratch_shapes=[
                 pltpu.VMEM((2 * len(distances), ROWS, HD), jnp.bfloat16),
                 pltpu.VMEM((2 * len(distances), HD, ROWS), jnp.bfloat16),
+                pltpu.VMEM((2, 2, ROWS, ROWS), jnp.float32),
             ],
             input_output_aliases={6: 0, 7: 1, 8: 2},
             compiler_params=params(),

time: 143 us -> 138 us (0.965)
  the two profiles are of different devices: /device:TPU:256 before, /device:TPU:96 now
where the time goes in v3:
time: 138 us; the launch traced here: 137 us
  blocking collectives  56.2 us (41%)
  starting transfers between devices  40.5 us (29%)
  waiting for transfers between devices  19 us (14%)
  Pallas kernels  15.5 us (11%)
  local copies, waits for them, and re-layouts  4.59 us (3%)
    all_to_all x1, blocking collectives, body(): pieces = lax.all_to_all(mixed.reshape(NX, 32, -1), 'x', 0, 0, tiled=True)  28.5 us
    all_to_all x1, blocking collectives, body(): parts = lax.all_to_all(packed, ('y', 'core'), 0, 0, tiled=True)  27.7 us
    ppermute x5, starting transfers between devices, body(): a[d] = lax.ppermute(send_a, 'z', [(i, (i + hops) % NZ) for i in range(NZ)])  25.8 us
    ppermute x5, waiting for transfers between devices, body(): a[d] = lax.ppermute(send_a, 'z', [(i, (i + hops) % NZ) for i in range(NZ)])  12.1 us
    pallas_call x5, Pallas kernels, body(): pl.pallas_call(functools.partial(step_kernel, distances, d == final), out...  10.6 us
    ppermute x4, starting transfers between devices, body(): b[d] = lax.ppermute(send_b, 'z', [(i, (i - hops) % NZ) for i in range(NZ)])  8.94 us
    ppermute x4, waiting for transfers between devices, body(): b[d] = lax.ppermute(send_b, 'z', [(i, (i - hops) % NZ) for i in range(NZ)])  6.62 us
    unnamed x14, local copies, waits for them, and re-layouts  4.58 us
  transfers between devices with their start and end apart: 13, of which 7 were waited for; matrix products, arithmetic and copies ran while one was open for 0% of the time, Pallas kernels for 9%

profile of v3, /device:TPU:96, one launch (start us, length us, event | category | flops | bytes accessed | tf_op | source)
XLA Modules:
  0.0 136.9 jit_solution(11683882035426925479)
XLA Ops:
  0.0 1.9 %collective-permute-start.12 = (bf16[512,4096]{1,0:T(8,128)(2,1)}, bf16[512,4096]{1,0:T(8,128)(2,1)S(1)}, u32[]{:S(2)}, u32[]{:S(2)}) collective-permute-start(bf16[512,4096]{1,0:T(8,128)(2,1)} %own_w_ref.1), channel_id=1, source_target_pairs={{0,1},{1,0},{2,3},{3,2},{4,5},{5,4},{6,7},{7,6},{8,9},{9,8},{10,11... | collective-permute-start | bytes 12582920 | tf_op jit(solution)/shard_map/ppermute | solution.py:303
  3.7 5.0 %collective-permute-start.3 = (bf16[256,256]{1,0:T(8,128)(2,1)S(1)}, bf16[256,256]{1,0:T(8,128)(2,1)S(1)}, u32[]{:S(2)}, u32[]{:S(2)}) collective-permute-start(bf16[256,256]{1,0:T(8,128)(2,1)S(1)} %pack.1.own_ref.b_ref), channel_id=1, source_target_pairs={{0,8},{8,16},{16,24},{24,32},{32,40},{40,48},{48,56},{56,64},{64,7... | collective-permute-start | bytes 393224 | tf_op jit(solution)/shard_map/ppermute | solution.py:291
  8.7 1.9 %collective-permute-start.8 = (bf16[256,256]{1,0:T(8,128)(2,1)S(1)}, bf16[256,256]{1,0:T(8,128)(2,1)S(1)}, u32[]{:S(2)}, u32[]{:S(2)}) collective-permute-start(bf16[256,256]{1,0:T(8,128)(2,1)S(1)} %pack.1.own_ref.b_ref), channel_id=1, source_target_pairs={{0,120},{8,0},{16,8},{24,16},{32,24},{40,32},{48,40},{56,48},{64,5... | collective-permute-start | bytes 393224 | tf_op jit(solution)/shard_map/ppermute | solution.py:296
  10.7 1.5 %collective-permute-done.3.a_ref = bf16[256,256]{1,0:T(8,128)(2,1)S(1)} collective-permute-done((bf16[256,256]{1,0:T(8,128)(2,1)S(1)}, bf16[256,256]{1,0:T(8,128)(2,1)S(1)}, u32[]{:S(2)}, u32[]{:S(2)}) %collective-permute-start.3) | collective-permute-done | bytes 131104 | tf_op jit(solution)/shard_map/ppermute | solution.py:291
  12.1 5.3 %collective-permute-done.8.b_ref = bf16[256,256]{1,0:T(8,128)(2,1)S(1)} collective-permute-done((bf16[256,256]{1,0:T(8,128)(2,1)S(1)}, bf16[256,256]{1,0:T(8,128)(2,1)S(1)}, u32[]{:S(2)}, u32[]{:S(2)}) %collective-permute-start.8) | collective-permute-done | bytes 131104 | tf_op jit(solution)/shard_map/ppermute | solution.py:296
  17.5 4.2 %collective-permute-start.4 = (bf16[512,256]{1,0:T(8,128)(2,1)S(1)}, bf16[512,256]{1,0:T(8,128)(2,1)S(1)}, u32[]{:S(2)}, u32[]{:S(2)}) collective-permute-start(bf16[512,256]{1,0:T(8,128)(2,1)S(1)} %get-tuple-element.42), channel_id=1, source_target_pairs={{0,16},{8,24},{16,32},{24,40},{32,48},{40,56},{48,64},{56,72},{64,... | collective-permute-start | bytes 786440 | tf_op jit(solution)/shard_map/ppermute | solution.py:291
  22.7 1.3 collective-permute-start
  24.0 2.6 %collective-permute-start.9 = (bf16[512,256]{1,0:T(8,128)(2,1)S(1)}, bf16[512,256]{1,0:T(8,128)(2,1)S(1)}, u32[]{:S(2)}, u32[]{:S(2)}) collective-permute-start(bf16[512,256]{1,0:T(8,128)(2,1)S(1)} %get-tuple-element.41), channel_id=1, source_target_pairs={{0,112},{8,120},{16,0},{24,8},{32,16},{40,24},{48,32},{56,40},{64,... | collective-permute-start | bytes 786440 | tf_op jit(solution)/shard_map/ppermute | solution.py:296
  26.6 6.8 %collective-permute-done.4.a_ref = bf16[512,256]{1,0:T(8,128)(2,1)S(1)} collective-permute-done((bf16[512,256]{1,0:T(8,128)(2,1)S(1)}, bf16[512,256]{1,0:T(8,128)(2,1)S(1)}, u32[]{:S(2)}, u32[]{:S(2)}) %collective-permute-start.4) | collective-permute-done | bytes 262176 | tf_op jit(solution)/shard_map/ppermute | solution.py:291
  33.3 5.4 %collective-permute-start.5 = (bf16[512,256]{1,0:T(8,128)(2,1)S(1)}, bf16[512,256]{1,0:T(8,128)(2,1)S(1)}, u32[]{:S(2)}, u32[]{:S(2)}) collective-permute-start(bf16[512,256]{1,0:T(8,128)(2,1)S(1)} %collective-permute-done.4.a_ref), channel_id=1, source_target_pairs={{0,16},{8,24},{16,32},{24,40},{32,48},{40,56},{48,64},{56,72},{64,... | collective-permute-start | bytes 786440 | tf_op jit(solution)/shard_map/ppermute | solution.py:291
  38.7 1.3 collective-permute-start.1
  40.0 1.3 collective-permute-start.2
  42.6 1.9 %collective-permute-start.10 = (bf16[512,256]{1,0:T(8,128)(2,1)S(1)}, bf16[512,256]{1,0:T(8,128)(2,1)S(1)}, u32[]{:S(2)}, u32[]{:S(2)}) collective-permute-start(bf16[512,256]{1,0:T(8,128)(2,1)S(1)} %collective-permute-done.9.b_ref), channel_id=1, source_target_pairs={{0,112},{8,120},{16,0},{24,8},{32,16},{40,24},{48,32},{56,40},{64,... | collective-permute-start | bytes 786440 | tf_op jit(solution)/shard_map/ppermute | solution.py:296
  44.5 3.3 %collective-permute-done.5.a_ref = bf16[512,256]{1,0:T(8,128)(2,1)S(1)} collective-permute-done((bf16[512,256]{1,0:T(8,128)(2,1)S(1)}, bf16[512,256]{1,0:T(8,128)(2,1)S(1)}, u32[]{:S(2)}, u32[]{:S(2)}) %collective-permute-start.5) | collective-permute-done | bytes 262176 | tf_op jit(solution)/shard_map/ppermute | solution.py:291
  47.8 4.0 %collective-permute-start.6 = (bf16[512,256]{1,0:T(8,128)(2,1)S(1)}, bf16[512,256]{1,0:T(8,128)(2,1)S(1)}, u32[]{:S(2)}, u32[]{:S(2)}) collective-permute-start(bf16[512,256]{1,0:T(8,128)(2,1)S(1)} %collective-permute-done.5.a_ref), channel_id=1, source_target_pairs={{0,16},{8,24},{16,32},{24,40},{32,48},{40,56},{48,64},{56,72},{64,... | collective-permute-start | bytes 786440 | tf_op jit(solution)/shard_map/ppermute | solution.py:291
  53.8 1.6 %first.1 = (f32[4,4,128,256]{3,2,1,0:T(8,128)S(1)}, f32[4,4,8,256]{3,2,1,0:T(8,128)S(1)}, f32[4,4,8,256]{3,2,1,0:T(8,128)S(1)}) custom-call(s32[8]{0:T(128)S(1)} %copy-done.4, s32[8]{0:T(128)S(1)} %copy-done.5, s32[8]{0:T(128)S(1)} %copy-done.6, bf16[1,256,512]{2,1,0:T(8,128)(2,1)S(1)} %bitcast.3, bf16[256,256]{1,0:T(8,128)(2,1)S(1)} %pack.1.own_ref.b_ref), custom_call_target="tpu_custom_call" | custom-call | flops 1073741824 | bytes 8388608 | tf_op jit(solution)/shard_map/first/pallas_call | solution.py:273
  55.7 2.5 %collective-permute-start.11 = (bf16[512,256]{1,0:T(8,128)(2,1)S(1)}, bf16[512,256]{1,0:T(8,128)(2,1)S(1)}, u32[]{:S(2)}, u32[]{:S(2)}) collective-permute-start(bf16[512,256]{1,0:T(8,128)(2,1)S(1)} %collective-permute-done.10.b_ref), channel_id=1, source_target_pairs={{0,112},{8,120},{16,0},{24,8},{32,16},{40,24},{48,32},{56,40},{64,... | collective-permute-start | bytes 786440 | tf_op jit(solution)/shard_map/ppermute | solution.py:296
  58.2 1.6 %step.5 = (f32[4,4,128,256]{3,2,1,0:T(8,128)S(1)}, f32[4,4,8,256]{3,2,1,0:T(8,128)S(1)}, f32[4,4,8,256]{3,2,1,0:T(8,128)S(1)}) custom-call(s32[8]{0:T(128)S(1)} %copy-done.4, s32[8]{0:T(128)S(1)} %copy-done.5, s32[8]{0:T(128)S(1)} %copy-done.6, bf16[4,256,512]{2,1,0:T(8,128)(2,1)S(1)} %stack.1.q_ref, ...), custom_call_target="tpu_custom_call", output_to_operand_aliasing={{0}: (6, {}), {1}: (7, {}), {2}: (8, {})} | custom-call | flops 1073741824 | bytes 8388608 | tf_op jit(solution)/shard_map/step/pallas_call | solution.py:314
  59.9 5.2 %step.6 = (f32[4,4,128,256]{3,2,1,0:T(8,128)S(1)}, f32[4,4,8,256]{3,2,1,0:T(8,128)S(1)}, f32[4,4,8,256]{3,2,1,0:T(8,128)S(1)}) custom-call(s32[8]{0:T(128)S(1)} %copy-done.4, s32[8]{0:T(128)S(1)} %copy-done.5, s32[8]{0:T(128)S(1)} %copy-done.6, bf16[4,256,512]{2,1,0:T(8,128)(2,1)S(1)} %stack.1.q_ref, ...), custom_call_target="tpu_custom_call", output_to_operand_aliasing={{0}: (6, {}), {1}: (7, {}), {2}: (8, {})} | custom-call | flops 1073741824 | bytes 8388608 | tf_op jit(solution)/shard_map/step/pallas_call | solution.py:314
  65.1 7.2 %collective-permute-start.7 = (bf16[256,256]{1,0:T(8,128)(2,1)S(1)}, bf16[256,256]{1,0:T(8,128)(2,1)S(1)}, u32[]{:S(2)}, u32[]{:S(2)}) collective-permute-start(bf16[256,256]{1,0:T(8,128)(2,1)S(1)} %slice.4), channel_id=1, source_target_pairs={{0,8},{8,16},{16,24},{24,32},{32,40},{40,48},{48,56},{56,64},{64,7... | collective-permute-start | bytes 393224 | tf_op jit(solution)/shard_map/ppermute | solution.py:291
  72.3 1.9 %step.7 = (f32[4,4,128,256]{3,2,1,0:T(8,128)S(1)}, f32[4,4,8,256]{3,2,1,0:T(8,128)S(1)}, f32[4,4,8,256]{3,2,1,0:T(8,128)S(1)}) custom-call(s32[8]{0:T(128)S(1)} %copy-done.4, s32[8]{0:T(128)S(1)} %copy-done.5, s32[8]{0:T(128)S(1)} %copy-done.6, bf16[4,256,512]{2,1,0:T(8,128)(2,1)S(1)} %stack.1.q_ref, ...), custom_call_target="tpu_custom_call", output_to_operand_aliasing={{0}: (6, {}), {1}: (7, {}), {2}: (8, {})} | custom-call | flops 1073741824 | bytes 8388608 | tf_op jit(solution)/shard_map/step/pallas_call | solution.py:314
  77.0 27.7 %all_to_all.10.parts_ref = bf16[8,528,128]{2,1,0:T(8,128)(2,1)S(1)} all-to-all(bf16[8,528,128]{2,1,0:T(8,128)(2,1)S(1)} %finish.1), channel_id=1, replica_groups=mesh['y'=4,'z'=16,'x'=4,'core'=2] {'y','core'}, dimensions={0} | all-to-all | bytes 2162688 | tf_op jit(solution)/shard_map/all_to_all | solution.py:338
  104.7 2.8 %project.1 = bf16[128,4096]{1,0:T(8,128)(2,1)S(1)} custom-call(bf16[8,528,128]{2,1,0:T(8,128)(2,1)S(1)} %all_to_all.10.parts_ref, bf16[512,4096]{1,0:T(8,128)(2,1)S(1)} %copy-done, bf16[512,4096]{1,0:T(8,128)(2,1)S(1)} %collective-permute-done.12.other_w_ref), custom_call_target="tpu_custom_call" | custom-call | tf_op jit(solution)/shard_map/project/pallas_call | solution.py:341
  107.5 28.5 %all_to_all.11 = bf16[4,32,4096]{2,1,0:T(8,128)(2,1)S(1)} all-to-all(bf16[4,32,4096]{2,1,0:T(8,128)(2,1)S(1)} %bitcast.2), channel_id=1, replica_groups=mesh['y'=4,'z'=16,'x'=4,'core'=2] {'x'}, dimensions={0} | all-to-all | bytes 2097152 | tf_op jit(solution)/shard_map/all_to_all | solution.py:355
  (32 shorter events, 10.0 us)
Async XLA Ops:
  0.0 104.7 %collective-permute-start.12 = (bf16[512,4096]{1,0:T(8,128)(2,1)}, bf16[512,4096]{1,0:T(8,128)(2,1)S(1)}, u32[]{:S(2)}, u32[]{:S(2)}) collective-permute-start(bf16[512,4096]{1,0:T(8,128)(2,1)} %own_w_ref.1), channel_id=1, source_target_pairs={{0,1},{1,0},{2,3},{3,2},{4,5},{5,4},{6,7},{7,6},{8,9},{9,8},{10,11... | collective-permute-start | bytes 12582920 | tf_op jit(solution)/shard_map/ppermute | solution.py:303
  1.9 0.8 copy-start.2
  2.8 0.8 copy-start.3
  3.7 8.4 %collective-permute-start.3 = (bf16[256,256]{1,0:T(8,128)(2,1)S(1)}, bf16[256,256]{1,0:T(8,128)(2,1)S(1)}, u32[]{:S(2)}, u32[]{:S(2)}) collective-permute-start(bf16[256,256]{1,0:T(8,128)(2,1)S(1)} %pack.1.own_ref.b_ref), channel_id=1, source_target_pairs={{0,8},{8,16},{16,24},{24,32},{32,40},{40,48},{48,56},{56,64},{64,7... | collective-permute-start | bytes 393224 | tf_op jit(solution)/shard_map/ppermute | solution.py:291
  8.7 8.7 %collective-permute-start.8 = (bf16[256,256]{1,0:T(8,128)(2,1)S(1)}, bf16[256,256]{1,0:T(8,128)(2,1)S(1)}, u32[]{:S(2)}, u32[]{:S(2)}) collective-permute-start(bf16[256,256]{1,0:T(8,128)(2,1)S(1)} %pack.1.own_ref.b_ref), channel_id=1, source_target_pairs={{0,120},{8,0},{16,8},{24,16},{32,24},{40,32},{48,40},{56,48},{64,5... | collective-permute-start | bytes 393224 | tf_op jit(solution)/shard_map/ppermute | solution.py:296
  17.5 15.8 %collective-permute-start.4 = (bf16[512,256]{1,0:T(8,128)(2,1)S(1)}, bf16[512,256]{1,0:T(8,128)(2,1)S(1)}, u32[]{:S(2)}, u32[]{:S(2)}) collective-permute-start(bf16[512,256]{1,0:T(8,128)(2,1)S(1)} %get-tuple-element.42), channel_id=1, source_target_pairs={{0,16},{8,24},{16,32},{24,40},{32,48},{40,56},{48,64},{56,72},{64,... | collective-permute-start | bytes 786440 | tf_op jit(solution)/shard_map/ppermute | solution.py:291
  21.7 1.0 copy-start.1
  22.7 17.3 %collective-permute-start = (bf16[256,512]{1,0:T(8,128)(2,1)S(1)}, bf16[256,512]{1,0:T(8,128)(2,1)S(1)}, u32[]{:S(2)}, u32[]{:S(2)}) collective-permute-start(bf16[256,512]{1,0:T(8,128)(2,1)S(1)} %order.1.q0_ref), channel_id=1, source_target_pairs={{128,0},{256,128},{384,256},{129,1},{257,129},{385,257},{130,2},{2... | collective-permute-start | bytes 786440 | tf_op jit(solution)/shard_map/ppermute | solution.py:302
  24.0 18.6 %collective-permute-start.9 = (bf16[512,256]{1,0:T(8,128)(2,1)S(1)}, bf16[512,256]{1,0:T(8,128)(2,1)S(1)}, u32[]{:S(2)}, u32[]{:S(2)}) collective-permute-start(bf16[512,256]{1,0:T(8,128)(2,1)S(1)} %get-tuple-element.41), channel_id=1, source_target_pairs={{0,112},{8,120},{16,0},{24,8},{32,16},{40,24},{48,32},{56,40},{64,... | collective-permute-start | bytes 786440 | tf_op jit(solution)/shard_map/ppermute | solution.py:296
  33.3 14.5 %collective-permute-start.5 = (bf16[512,256]{1,0:T(8,128)(2,1)S(1)}, bf16[512,256]{1,0:T(8,128)(2,1)S(1)}, u32[]{:S(2)}, u32[]{:S(2)}) collective-permute-start(bf16[512,256]{1,0:T(8,128)(2,1)S(1)} %collective-permute-done.4.a_ref), channel_id=1, source_target_pairs={{0,16},{8,24},{16,32},{24,40},{32,48},{40,56},{48,64},{56,72},{64,... | collective-permute-start | bytes 786440 | tf_op jit(solution)/shard_map/ppermute | solution.py:291
  38.7 16.7 %collective-permute-start.1 = (bf16[256,512]{1,0:T(8,128)(2,1)S(1)}, bf16[256,512]{1,0:T(8,128)(2,1)S(1)}, u32[]{:S(2)}, u32[]{:S(2)}) collective-permute-start(bf16[256,512]{1,0:T(8,128)(2,1)S(1)} %order.1.q0_ref), channel_id=1, source_target_pairs={{256,0},{384,128},{257,1},{385,129},{258,2},{386,130},{259,3},{387... | collective-permute-start | bytes 786440 | tf_op jit(solution)/shard_map/ppermute | solution.py:302
  40.0 15.6 %collective-permute-start.2 = (bf16[256,512]{1,0:T(8,128)(2,1)S(1)}, bf16[256,512]{1,0:T(8,128)(2,1)S(1)}, u32[]{:S(2)}, u32[]{:S(2)}) collective-permute-start(bf16[256,512]{1,0:T(8,128)(2,1)S(1)} %order.1.q0_ref), channel_id=1, source_target_pairs={{384,0},{385,1},{386,2},{387,3},{388,4},{389,5},{390,6},{391,7},{3... | collective-permute-start | bytes 786440 | tf_op jit(solution)/shard_map/ppermute | solution.py:302
  42.6 13.1 %collective-permute-start.10 = (bf16[512,256]{1,0:T(8,128)(2,1)S(1)}, bf16[512,256]{1,0:T(8,128)(2,1)S(1)}, u32[]{:S(2)}, u32[]{:S(2)}) collective-permute-start(bf16[512,256]{1,0:T(8,128)(2,1)S(1)} %collective-permute-done.9.b_ref), channel_id=1, source_target_pairs={{0,112},{8,120},{16,0},{24,8},{32,16},{40,24},{48,32},{56,40},{64,... | collective-permute-start | bytes 786440 | tf_op jit(solution)/shard_map/ppermute | solution.py:296
  47.8 17.3 %collective-permute-start.6 = (bf16[512,256]{1,0:T(8,128)(2,1)S(1)}, bf16[512,256]{1,0:T(8,128)(2,1)S(1)}, u32[]{:S(2)}, u32[]{:S(2)}) collective-permute-start(bf16[512,256]{1,0:T(8,128)(2,1)S(1)} %collective-permute-done.5.a_ref), channel_id=1, source_target_pairs={{0,16},{8,24},{16,32},{24,40},{32,48},{40,56},{48,64},{56,72},{64,... | collective-permute-start | bytes 786440 | tf_op jit(solution)/shard_map/ppermute | solution.py:291
  51.8 0.7 copy-start.4
  52.5 0.7 copy-start.5
  53.2 0.7 copy-start.6
  55.7 18.5 %collective-permute-start.11 = (bf16[512,256]{1,0:T(8,128)(2,1)S(1)}, bf16[512,256]{1,0:T(8,128)(2,1)S(1)}, u32[]{:S(2)}, u32[]{:S(2)}) collective-permute-start(bf16[512,256]{1,0:T(8,128)(2,1)S(1)} %collective-permute-done.10.b_ref), channel_id=1, source_target_pairs={{0,112},{8,120},{16,0},{24,8},{32,16},{40,24},{48,32},{56,40},{64,... | collective-permute-start | bytes 786440 | tf_op jit(solution)/shard_map/ppermute | solution.py:296
  65.1 10.8 %collective-permute-start.7 = (bf16[256,256]{1,0:T(8,128)(2,1)S(1)}, bf16[256,256]{1,0:T(8,128)(2,1)S(1)}, u32[]{:S(2)}, u32[]{:S(2)}) collective-permute-start(bf16[256,256]{1,0:T(8,128)(2,1)S(1)} %slice.4), channel_id=1, source_target_pairs={{0,8},{8,16},{16,24},{24,32},{32,40},{40,48},{48,56},{56,64},{64,7... | collective-permute-start | bytes 393224 | tf_op jit(solution)/shard_map/ppermute | solution.py:291
  76.7 28.0 %copy-start = (bf16[512,4096]{1,0:T(8,128)(2,1)S(1)}, bf16[512,4096]{1,0:T(8,128)(2,1)}, u32[]{:S(2)}) copy-start(bf16[512,4096]{1,0:T(8,128)(2,1)} %own_w_ref.1) | copy-start | bytes 12582916

commit v4 on v3

--- a/solution.py
+++ b/solution.py
@@ -147,11 +147,10 @@
 
         @pl.loop(jnp.where(any_before, 0, 1), slots)
         def _(slot):
-            for i in range(0, len(places), 2):
-                sides = (i, i + 1)
-                valid = [(slot > 0) | before[n] for n in sides]
-                keys, values = [k_ref[n] for n in sides], [v_ref[n] for n in sides]
-                fold(q_ref, slot, keys, values, None, valid, acc, top, total, s_ref)
+            sides = range(len(places))
+            valid = [(slot > 0) | before[n] for n in sides]
+            keys, values = [k_ref[n] for n in sides], [v_ref[n] for n in sides]
+            fold(q_ref, slot, keys, values, None, valid, acc, top, total, s_ref)
 
     @pl.when(kind != 1)
     def _():
@@ -246,6 +245,7 @@
 
 
 ROUNDS = {1: (1, (1,)), 2: (2, (2, 3)), 3: (2, (4, 5)), 4: (2, (6, 7)), 5: (1, (8,))}
+FOLDS = (2, 1, 3, 4, 5)
 
 
 def body(queries, keys, values, head_kind, sink_len, window_len, w_out):
@@ -310,7 +310,8 @@
         compiler_params=params(),
         name="stack",
     )(queries, *received)
-    for d, (_, distances) in ROUNDS.items():
+    for d in FOLDS:
+        distances = ROUNDS[d][1]
         state = pl.pallas_call(
             functools.partial(step_kernel, distances, d == final),
             out_shape=STATE,
@@ -319,7 +320,7 @@
             scratch_shapes=[
                 pltpu.VMEM((2 * len(distances), ROWS, HD), jnp.bfloat16),
                 pltpu.VMEM((2 * len(distances), HD, ROWS), jnp.bfloat16),
-                pltpu.VMEM((2, 2, ROWS, ROWS), jnp.float32),
+                pltpu.VMEM((2, 2 * len(distances), ROWS, ROWS), jnp.float32),
             ],
             input_output_aliases={6: 0, 7: 1, 8: 2},
             compiler_params=params(),

time: 138 us -> 134 us (0.971)
  blocking collectives: 56.2 us -> 53 us
    all_to_all x1, blocking collectives: 27.7 us -> 24.5 us  [body(): parts = lax.all_to_all(packed, ('y', 'core'), 0, 0, tiled=True)]
where the time goes in v4:
time: 134 us; the launch traced here: 133 us
  blocking collectives  53 us (40%)
  starting transfers between devices  40.5 us (30%)
  waiting for transfers between devices  18.7 us (14%)
  Pallas kernels  15.5 us (12%)
  local copies, waits for them, and re-layouts  4.59 us (3%)
    all_to_all x1, blocking collectives, body(): pieces = lax.all_to_all(mixed.reshape(NX, 32, -1), 'x', 0, 0, tiled=True)  28.5 us
    ppermute x5, starting transfers between devices, body(): a[d] = lax.ppermute(send_a, 'z', [(i, (i + hops) % NZ) for i in range(NZ)])  25.8 us
    all_to_all x1, blocking collectives, body(): parts = lax.all_to_all(packed, ('y', 'core'), 0, 0, tiled=True)  24.5 us
    ppermute x5, waiting for transfers between devices, body(): a[d] = lax.ppermute(send_a, 'z', [(i, (i + hops) % NZ) for i in range(NZ)])  11.9 us
    pallas_call x5, Pallas kernels, body(): pl.pallas_call(functools.partial(step_kernel, distances, d == final), out...  10.6 us
    ppermute x4, starting transfers between devices, body(): b[d] = lax.ppermute(send_b, 'z', [(i, (i - hops) % NZ) for i in range(NZ)])  8.94 us
    ppermute x4, waiting for transfers between devices, body(): b[d] = lax.ppermute(send_b, 'z', [(i, (i - hops) % NZ) for i in range(NZ)])  6.62 us
    unnamed x14, local copies, waits for them, and re-layouts  4.58 us
  transfers between devices with their start and end apart: 13, of which 7 were waited for; matrix products, arithmetic and copies ran while one was open for 0% of the time, Pallas kernels for 9%

profile of v4, /device:TPU:96, one launch (start us, length us, event | category | flops | bytes accessed | tf_op | source)
XLA Modules:
  0.0 133.4 jit_solution(8513195016051428849)
XLA Ops:
  0.0 1.9 %collective-permute-start.12 = (bf16[512,4096]{1,0:T(8,128)(2,1)}, bf16[512,4096]{1,0:T(8,128)(2,1)S(1)}, u32[]{:S(2)}, u32[]{:S(2)}) collective-permute-start(bf16[512,4096]{1,0:T(8,128)(2,1)} %own_w_ref.1), channel_id=1, source_target_pairs={{0,1},{1,0},{2,3},{3,2},{4,5},{5,4},{6,7},{7,6},{8,9},{9,8},{10,11... | collective-permute-start | bytes 12582920 | tf_op jit(solution)/shard_map/ppermute | solution.py:303
  3.7 5.0 %collective-permute-start.3 = (bf16[256,256]{1,0:T(8,128)(2,1)S(1)}, bf16[256,256]{1,0:T(8,128)(2,1)S(1)}, u32[]{:S(2)}, u32[]{:S(2)}) collective-permute-start(bf16[256,256]{1,0:T(8,128)(2,1)S(1)} %pack.1.own_ref.b_ref), channel_id=1, source_target_pairs={{0,8},{8,16},{16,24},{24,32},{32,40},{40,48},{48,56},{56,64},{64,7... | collective-permute-start | bytes 393224 | tf_op jit(solution)/shard_map/ppermute | solution.py:291
  8.7 1.9 %collective-permute-start.8 = (bf16[256,256]{1,0:T(8,128)(2,1)S(1)}, bf16[256,256]{1,0:T(8,128)(2,1)S(1)}, u32[]{:S(2)}, u32[]{:S(2)}) collective-permute-start(bf16[256,256]{1,0:T(8,128)(2,1)S(1)} %pack.1.own_ref.b_ref), channel_id=1, source_target_pairs={{0,120},{8,0},{16,8},{24,16},{32,24},{40,32},{48,40},{56,48},{64,5... | collective-permute-start | bytes 393224 | tf_op jit(solution)/shard_map/ppermute | solution.py:296
  10.7 1.5 %collective-permute-done.3.a_ref = bf16[256,256]{1,0:T(8,128)(2,1)S(1)} collective-permute-done((bf16[256,256]{1,0:T(8,128)(2,1)S(1)}, bf16[256,256]{1,0:T(8,128)(2,1)S(1)}, u32[]{:S(2)}, u32[]{:S(2)}) %collective-permute-start.3) | collective-permute-done | bytes 131104 | tf_op jit(solution)/shard_map/ppermute | solution.py:291
  12.1 5.3 %collective-permute-done.8.b_ref = bf16[256,256]{1,0:T(8,128)(2,1)S(1)} collective-permute-done((bf16[256,256]{1,0:T(8,128)(2,1)S(1)}, bf16[256,256]{1,0:T(8,128)(2,1)S(1)}, u32[]{:S(2)}, u32[]{:S(2)}) %collective-permute-start.8) | collective-permute-done | bytes 131104 | tf_op jit(solution)/shard_map/ppermute | solution.py:296
  17.5 4.2 %collective-permute-start.4 = (bf16[512,256]{1,0:T(8,128)(2,1)S(1)}, bf16[512,256]{1,0:T(8,128)(2,1)S(1)}, u32[]{:S(2)}, u32[]{:S(2)}) collective-permute-start(bf16[512,256]{1,0:T(8,128)(2,1)S(1)} %get-tuple-element.42), channel_id=1, source_target_pairs={{0,16},{8,24},{16,32},{24,40},{32,48},{40,56},{48,64},{56,72},{64,... | collective-permute-start | bytes 786440 | tf_op jit(solution)/shard_map/ppermute | solution.py:291
  22.7 1.3 collective-permute-start
  24.0 2.6 %collective-permute-start.9 = (bf16[512,256]{1,0:T(8,128)(2,1)S(1)}, bf16[512,256]{1,0:T(8,128)(2,1)S(1)}, u32[]{:S(2)}, u32[]{:S(2)}) collective-permute-start(bf16[512,256]{1,0:T(8,128)(2,1)S(1)} %get-tuple-element.41), channel_id=1, source_target_pairs={{0,112},{8,120},{16,0},{24,8},{32,16},{40,24},{48,32},{56,40},{64,... | collective-permute-start | bytes 786440 | tf_op jit(solution)/shard_map/ppermute | solution.py:296
  26.6 6.8 %collective-permute-done.4.a_ref = bf16[512,256]{1,0:T(8,128)(2,1)S(1)} collective-permute-done((bf16[512,256]{1,0:T(8,128)(2,1)S(1)}, bf16[512,256]{1,0:T(8,128)(2,1)S(1)}, u32[]{:S(2)}, u32[]{:S(2)}) %collective-permute-start.4) | collective-permute-done | bytes 262176 | tf_op jit(solution)/shard_map/ppermute | solution.py:291
  33.3 5.4 %collective-permute-start.5 = (bf16[512,256]{1,0:T(8,128)(2,1)S(1)}, bf16[512,256]{1,0:T(8,128)(2,1)S(1)}, u32[]{:S(2)}, u32[]{:S(2)}) collective-permute-start(bf16[512,256]{1,0:T(8,128)(2,1)S(1)} %collective-permute-done.4.a_ref), channel_id=1, source_target_pairs={{0,16},{8,24},{16,32},{24,40},{32,48},{40,56},{48,64},{56,72},{64,... | collective-permute-start | bytes 786440 | tf_op jit(solution)/shard_map/ppermute | solution.py:291
  38.7 1.3 collective-permute-start.1
  40.0 1.3 collective-permute-start.2
  42.6 1.9 %collective-permute-start.10 = (bf16[512,256]{1,0:T(8,128)(2,1)S(1)}, bf16[512,256]{1,0:T(8,128)(2,1)S(1)}, u32[]{:S(2)}, u32[]{:S(2)}) collective-permute-start(bf16[512,256]{1,0:T(8,128)(2,1)S(1)} %collective-permute-done.9.b_ref), channel_id=1, source_target_pairs={{0,112},{8,120},{16,0},{24,8},{32,16},{40,24},{48,32},{56,40},{64,... | collective-permute-start | bytes 786440 | tf_op jit(solution)/shard_map/ppermute | solution.py:296
  44.5 3.3 %collective-permute-done.5.a_ref = bf16[512,256]{1,0:T(8,128)(2,1)S(1)} collective-permute-done((bf16[512,256]{1,0:T(8,128)(2,1)S(1)}, bf16[512,256]{1,0:T(8,128)(2,1)S(1)}, u32[]{:S(2)}, u32[]{:S(2)}) %collective-permute-start.5) | collective-permute-done | bytes 262176 | tf_op jit(solution)/shard_map/ppermute | solution.py:291
  47.8 4.0 %collective-permute-start.6 = (bf16[512,256]{1,0:T(8,128)(2,1)S(1)}, bf16[512,256]{1,0:T(8,128)(2,1)S(1)}, u32[]{:S(2)}, u32[]{:S(2)}) collective-permute-start(bf16[512,256]{1,0:T(8,128)(2,1)S(1)} %collective-permute-done.5.a_ref), channel_id=1, source_target_pairs={{0,16},{8,24},{16,32},{24,40},{32,48},{40,56},{48,64},{56,72},{64,... | collective-permute-start | bytes 786440 | tf_op jit(solution)/shard_map/ppermute | solution.py:291
  53.8 1.6 %first.1 = (f32[4,4,128,256]{3,2,1,0:T(8,128)S(1)}, f32[4,4,8,256]{3,2,1,0:T(8,128)S(1)}, f32[4,4,8,256]{3,2,1,0:T(8,128)S(1)}) custom-call(s32[8]{0:T(128)S(1)} %copy-done.4, s32[8]{0:T(128)S(1)} %copy-done.5, s32[8]{0:T(128)S(1)} %copy-done.6, bf16[1,256,512]{2,1,0:T(8,128)(2,1)S(1)} %bitcast.3, bf16[256,256]{1,0:T(8,128)(2,1)S(1)} %pack.1.own_ref.b_ref), custom_call_target="tpu_custom_call" | custom-call | flops 1073741824 | bytes 8388608 | tf_op jit(solution)/shard_map/first/pallas_call | solution.py:273
  55.7 2.5 %collective-permute-start.11 = (bf16[512,256]{1,0:T(8,128)(2,1)S(1)}, bf16[512,256]{1,0:T(8,128)(2,1)S(1)}, u32[]{:S(2)}, u32[]{:S(2)}) collective-permute-start(bf16[512,256]{1,0:T(8,128)(2,1)S(1)} %collective-permute-done.10.b_ref), channel_id=1, source_target_pairs={{0,112},{8,120},{16,0},{24,8},{32,16},{40,24},{48,32},{56,40},{64,... | collective-permute-start | bytes 786440 | tf_op jit(solution)/shard_map/ppermute | solution.py:296
  58.2 5.2 %step.5 = (f32[4,4,128,256]{3,2,1,0:T(8,128)S(1)}, f32[4,4,8,256]{3,2,1,0:T(8,128)S(1)}, f32[4,4,8,256]{3,2,1,0:T(8,128)S(1)}) custom-call(s32[8]{0:T(128)S(1)} %copy-done.4, s32[8]{0:T(128)S(1)} %copy-done.5, s32[8]{0:T(128)S(1)} %copy-done.6, bf16[4,256,512]{2,1,0:T(8,128)(2,1)S(1)} %stack.1.q_ref, ...), custom_call_target="tpu_custom_call", output_to_operand_aliasing={{0}: (6, {}), {1}: (7, {}), {2}: (8, {})} | custom-call | flops 1073741824 | bytes 8388608 | tf_op jit(solution)/shard_map/step/pallas_call | solution.py:315
  63.4 1.6 %step.6 = (f32[4,4,128,256]{3,2,1,0:T(8,128)S(1)}, f32[4,4,8,256]{3,2,1,0:T(8,128)S(1)}, f32[4,4,8,256]{3,2,1,0:T(8,128)S(1)}) custom-call(s32[8]{0:T(128)S(1)} %copy-done.4, s32[8]{0:T(128)S(1)} %copy-done.5, s32[8]{0:T(128)S(1)} %copy-done.6, bf16[4,256,512]{2,1,0:T(8,128)(2,1)S(1)} %stack.1.q_ref, ...), custom_call_target="tpu_custom_call", output_to_operand_aliasing={{0}: (6, {}), {1}: (7, {}), {2}: (8, {})} | custom-call | flops 1073741824 | bytes 8388608 | tf_op jit(solution)/shard_map/step/pallas_call | solution.py:315
  65.1 7.2 %collective-permute-start.7 = (bf16[256,256]{1,0:T(8,128)(2,1)S(1)}, bf16[256,256]{1,0:T(8,128)(2,1)S(1)}, u32[]{:S(2)}, u32[]{:S(2)}) collective-permute-start(bf16[256,256]{1,0:T(8,128)(2,1)S(1)} %slice.4), channel_id=1, source_target_pairs={{0,8},{8,16},{16,24},{24,32},{32,40},{40,48},{48,56},{56,64},{64,7... | collective-permute-start | bytes 393224 | tf_op jit(solution)/shard_map/ppermute | solution.py:291
  72.3 1.9 %step.7 = (f32[4,4,128,256]{3,2,1,0:T(8,128)S(1)}, f32[4,4,8,256]{3,2,1,0:T(8,128)S(1)}, f32[4,4,8,256]{3,2,1,0:T(8,128)S(1)}) custom-call(s32[8]{0:T(128)S(1)} %copy-done.4, s32[8]{0:T(128)S(1)} %copy-done.5, s32[8]{0:T(128)S(1)} %copy-done.6, bf16[4,256,512]{2,1,0:T(8,128)(2,1)S(1)} %stack.1.q_ref, ...), custom_call_target="tpu_custom_call", output_to_operand_aliasing={{0}: (6, {}), {1}: (7, {}), {2}: (8, {})} | custom-call | flops 1073741824 | bytes 8388608 | tf_op jit(solution)/shard_map/step/pallas_call | solution.py:315
  76.7 24.5 %all_to_all.10.parts_ref = bf16[8,528,128]{2,1,0:T(8,128)(2,1)S(1)} all-to-all(bf16[8,528,128]{2,1,0:T(8,128)(2,1)S(1)} %finish.1), channel_id=1, replica_groups=mesh['y'=4,'z'=16,'x'=4,'core'=2] {'y','core'}, dimensions={0} | all-to-all | bytes 2162688 | tf_op jit(solution)/shard_map/all_to_all | solution.py:339
  101.2 2.8 %project.1 = bf16[128,4096]{1,0:T(8,128)(2,1)S(1)} custom-call(bf16[8,528,128]{2,1,0:T(8,128)(2,1)S(1)} %all_to_all.10.parts_ref, bf16[512,4096]{1,0:T(8,128)(2,1)S(1)} %copy-done, bf16[512,4096]{1,0:T(8,128)(2,1)S(1)} %collective-permute-done.12.other_w_ref), custom_call_target="tpu_custom_call" | custom-call | tf_op jit(solution)/shard_map/project/pallas_call | solution.py:342
  104.0 28.5 %all_to_all.11 = bf16[4,32,4096]{2,1,0:T(8,128)(2,1)S(1)} all-to-all(bf16[4,32,4096]{2,1,0:T(8,128)(2,1)S(1)} %bitcast.2), channel_id=1, replica_groups=mesh['y'=4,'z'=16,'x'=4,'core'=2] {'x'}, dimensions={0} | all-to-all | bytes 2097152 | tf_op jit(solution)/shard_map/all_to_all | solution.py:356
  (32 shorter events, 9.7 us)
Async XLA Ops:
  0.0 101.2 %collective-permute-start.12 = (bf16[512,4096]{1,0:T(8,128)(2,1)}, bf16[512,4096]{1,0:T(8,128)(2,1)S(1)}, u32[]{:S(2)}, u32[]{:S(2)}) collective-permute-start(bf16[512,4096]{1,0:T(8,128)(2,1)} %own_w_ref.1), channel_id=1, source_target_pairs={{0,1},{1,0},{2,3},{3,2},{4,5},{5,4},{6,7},{7,6},{8,9},{9,8},{10,11... | collective-permute-start | bytes 12582920 | tf_op jit(solution)/shard_map/ppermute | solution.py:303
  1.9 0.8 copy-start.2
  2.8 0.8 copy-start.3
  3.7 8.4 %collective-permute-start.3 = (bf16[256,256]{1,0:T(8,128)(2,1)S(1)}, bf16[256,256]{1,0:T(8,128)(2,1)S(1)}, u32[]{:S(2)}, u32[]{:S(2)}) collective-permute-start(bf16[256,256]{1,0:T(8,128)(2,1)S(1)} %pack.1.own_ref.b_ref), channel_id=1, source_target_pairs={{0,8},{8,16},{16,24},{24,32},{32,40},{40,48},{48,56},{56,64},{64,7... | collective-permute-start | bytes 393224 | tf_op jit(solution)/shard_map/ppermute | solution.py:291
  8.7 8.7 %collective-permute-start.8 = (bf16[256,256]{1,0:T(8,128)(2,1)S(1)}, bf16[256,256]{1,0:T(8,128)(2,1)S(1)}, u32[]{:S(2)}, u32[]{:S(2)}) collective-permute-start(bf16[256,256]{1,0:T(8,128)(2,1)S(1)} %pack.1.own_ref.b_ref), channel_id=1, source_target_pairs={{0,120},{8,0},{16,8},{24,16},{32,24},{40,32},{48,40},{56,48},{64,5... | collective-permute-start | bytes 393224 | tf_op jit(solution)/shard_map/ppermute | solution.py:296
  17.5 15.8 %collective-permute-start.4 = (bf16[512,256]{1,0:T(8,128)(2,1)S(1)}, bf16[512,256]{1,0:T(8,128)(2,1)S(1)}, u32[]{:S(2)}, u32[]{:S(2)}) collective-permute-start(bf16[512,256]{1,0:T(8,128)(2,1)S(1)} %get-tuple-element.42), channel_id=1, source_target_pairs={{0,16},{8,24},{16,32},{24,40},{32,48},{40,56},{48,64},{56,72},{64,... | collective-permute-start | bytes 786440 | tf_op jit(solution)/shard_map/ppermute | solution.py:291
  21.7 1.0 copy-start.1
  22.7 17.3 %collective-permute-start = (bf16[256,512]{1,0:T(8,128)(2,1)S(1)}, bf16[256,512]{1,0:T(8,128)(2,1)S(1)}, u32[]{:S(2)}, u32[]{:S(2)}) collective-permute-start(bf16[256,512]{1,0:T(8,128)(2,1)S(1)} %order.1.q0_ref), channel_id=1, source_target_pairs={{128,0},{256,128},{384,256},{129,1},{257,129},{385,257},{130,2},{2... | collective-permute-start | bytes 786440 | tf_op jit(solution)/shard_map/ppermute | solution.py:302
  24.0 18.6 %collective-permute-start.9 = (bf16[512,256]{1,0:T(8,128)(2,1)S(1)}, bf16[512,256]{1,0:T(8,128)(2,1)S(1)}, u32[]{:S(2)}, u32[]{:S(2)}) collective-permute-start(bf16[512,256]{1,0:T(8,128)(2,1)S(1)} %get-tuple-element.41), channel_id=1, source_target_pairs={{0,112},{8,120},{16,0},{24,8},{32,16},{40,24},{48,32},{56,40},{64,... | collective-permute-start | bytes 786440 | tf_op jit(solution)/shard_map/ppermute | solution.py:296
  33.3 14.5 %collective-permute-start.5 = (bf16[512,256]{1,0:T(8,128)(2,1)S(1)}, bf16[512,256]{1,0:T(8,128)(2,1)S(1)}, u32[]{:S(2)}, u32[]{:S(2)}) collective-permute-start(bf16[512,256]{1,0:T(8,128)(2,1)S(1)} %collective-permute-done.4.a_ref), channel_id=1, source_target_pairs={{0,16},{8,24},{16,32},{24,40},{32,48},{40,56},{48,64},{56,72},{64,... | collective-permute-start | bytes 786440 | tf_op jit(solution)/shard_map/ppermute | solution.py:291
  38.7 16.7 %collective-permute-start.1 = (bf16[256,512]{1,0:T(8,128)(2,1)S(1)}, bf16[256,512]{1,0:T(8,128)(2,1)S(1)}, u32[]{:S(2)}, u32[]{:S(2)}) collective-permute-start(bf16[256,512]{1,0:T(8,128)(2,1)S(1)} %order.1.q0_ref), channel_id=1, source_target_pairs={{256,0},{384,128},{257,1},{385,129},{258,2},{386,130},{259,3},{387... | collective-permute-start | bytes 786440 | tf_op jit(solution)/shard_map/ppermute | solution.py:302
  40.0 15.6 %collective-permute-start.2 = (bf16[256,512]{1,0:T(8,128)(2,1)S(1)}, bf16[256,512]{1,0:T(8,128)(2,1)S(1)}, u32[]{:S(2)}, u32[]{:S(2)}) collective-permute-start(bf16[256,512]{1,0:T(8,128)(2,1)S(1)} %order.1.q0_ref), channel_id=1, source_target_pairs={{384,0},{385,1},{386,2},{387,3},{388,4},{389,5},{390,6},{391,7},{3... | collective-permute-start | bytes 786440 | tf_op jit(solution)/shard_map/ppermute | solution.py:302
  42.6 13.1 %collective-permute-start.10 = (bf16[512,256]{1,0:T(8,128)(2,1)S(1)}, bf16[512,256]{1,0:T(8,128)(2,1)S(1)}, u32[]{:S(2)}, u32[]{:S(2)}) collective-permute-start(bf16[512,256]{1,0:T(8,128)(2,1)S(1)} %collective-permute-done.9.b_ref), channel_id=1, source_target_pairs={{0,112},{8,120},{16,0},{24,8},{32,16},{40,24},{48,32},{56,40},{64,... | collective-permute-start | bytes 786440 | tf_op jit(solution)/shard_map/ppermute | solution.py:296
  47.8 17.3 %collective-permute-start.6 = (bf16[512,256]{1,0:T(8,128)(2,1)S(1)}, bf16[512,256]{1,0:T(8,128)(2,1)S(1)}, u32[]{:S(2)}, u32[]{:S(2)}) collective-permute-start(bf16[512,256]{1,0:T(8,128)(2,1)S(1)} %collective-permute-done.5.a_ref), channel_id=1, source_target_pairs={{0,16},{8,24},{16,32},{24,40},{32,48},{40,56},{48,64},{56,72},{64,... | collective-permute-start | bytes 786440 | tf_op jit(solution)/shard_map/ppermute | solution.py:291
  51.8 0.7 copy-start.4
  52.5 0.7 copy-start.5
  53.2 0.7 copy-start.6
  55.7 18.5 %collective-permute-start.11 = (bf16[512,256]{1,0:T(8,128)(2,1)S(1)}, bf16[512,256]{1,0:T(8,128)(2,1)S(1)}, u32[]{:S(2)}, u32[]{:S(2)}) collective-permute-start(bf16[512,256]{1,0:T(8,128)(2,1)S(1)} %collective-permute-done.10.b_ref), channel_id=1, source_target_pairs={{0,112},{8,120},{16,0},{24,8},{32,16},{40,24},{48,32},{56,40},{64,... | collective-permute-start | bytes 786440 | tf_op jit(solution)/shard_map/ppermute | solution.py:296
  65.1 10.5 %collective-permute-start.7 = (bf16[256,256]{1,0:T(8,128)(2,1)S(1)}, bf16[256,256]{1,0:T(8,128)(2,1)S(1)}, u32[]{:S(2)}, u32[]{:S(2)}) collective-permute-start(bf16[256,256]{1,0:T(8,128)(2,1)S(1)} %slice.4), channel_id=1, source_target_pairs={{0,8},{8,16},{16,24},{24,32},{32,40},{40,48},{48,56},{56,64},{64,7... | collective-permute-start | bytes 393224 | tf_op jit(solution)/shard_map/ppermute | solution.py:291
  76.4 24.8 %copy-start = (bf16[512,4096]{1,0:T(8,128)(2,1)S(1)}, bf16[512,4096]{1,0:T(8,128)(2,1)}, u32[]{:S(2)}) copy-start(bf16[512,4096]{1,0:T(8,128)(2,1)} %own_w_ref.1) | copy-start | bytes 12582916
